TPU v7x, 32 devices: a whole 2x2x4 slice. The times are simulated.
32 devices in a mesh: gx: 2 (over y), gy: 4 (over z), gz: 4 (over x, core).
Axes of the slice: x: 2, y: 2, z: 4, core: 2. Of those that a mesh axis runs over, the one named last changes fastest.
Arguments:
- couplings: float32 [18, 16, 32, 512], P(None, 'gx', 'gy', 'gz'), may hold values from 0.05 to 2
- diagonal: float32 [3, 16, 32, 512], P(None, 'gx', 'gy', 'gz'), may hold values from 0.01 to 0.1
- right_side: float32 [3, 16, 32, 512], P(None, 'gx', 'gy', 'gz'), may hold values from -6 to 6
- guess: float32 [3, 16, 32, 512], P(None, 'gx', 'gy', 'gz'), may hold values from -4 to 4
Outputs:
- solution: float32 [3, 16, 32, 512], P(None, 'gx', 'gy', 'gz')
All inputs are finite; a program needn't handle non-finite values.
Results may differ from a plain program's by a relative error of at most 0.00011.
Values sent between devices are 32-bit elements; how exact they have to be, the bound alone decides.
A program may use at most 128 MiB of HBM per device.

v0:
```python
import jax
import jax.numpy as jnp
from jax import lax
from jax.sharding import PartitionSpec as P

LEVELS = 4
SWEEPS = 2
COARSE_SWEEPS = 8


damping = 0.8


def padded_2(block, sides, width):
    for axis, dim in sides:
        count = lax.axis_size(axis)
        forward = [(i, i + 1) for i in range(count - 1)]
        backward = [(target, source) for source, target in forward]
        low = lax.ppermute(
            lax.slice_in_dim(block, block.shape[dim] - width, None, axis=dim), axis, forward
        )
        high = lax.ppermute(lax.slice_in_dim(block, 0, width, axis=dim), axis, backward)
        block = jnp.concatenate([low, block, high], axis=dim)
    return block


def pad_zero(field):
    return jnp.pad(field, ((0, 0), (1, 1), (1, 1), (1, 1)))


def operate(field, padded, weights, total):
    near = [
        padded[:, 2:, 1:-1, 1:-1],
        padded[:, :-2, 1:-1, 1:-1],
        padded[:, 1:-1, 2:, 1:-1],
        padded[:, 1:-1, :-2, 1:-1],
        padded[:, 1:-1, 1:-1, 2:],
        padded[:, 1:-1, 1:-1, :-2],
    ]
    offdiag = weights[:, 0] * near[0]
    for index in range(1, 6):
        offdiag = offdiag + weights[:, index] * near[index]
    return total * field - offdiag


def coarsen(array):
    shape = array.shape
    count = len(shape)
    blocks = array.reshape(shape[:-3] + (shape[-3] // 2, 2, shape[-2] // 2, 2, shape[-1] // 2, 2))
    return jnp.mean(blocks, axis=(count - 2, count, count + 2))


def refine(array):
    return jnp.repeat(jnp.repeat(jnp.repeat(array, 2, axis=-3), 2, axis=-2), 2, axis=-1)


def hierarchy(couplings, diagonal):
    weights = couplings.reshape((3, 6) + diagonal.shape[1:])
    local_diag = diagonal
    result = []
    for level in range(LEVELS):
        if level > 0:
            weights = coarsen(weights) * 0.25
            local_diag = coarsen(local_diag)
        result.append((weights, local_diag + jnp.sum(weights, axis=1)))
    return result


def apply_brick(field, weights, total):
    padded = padded_2(field, (("gx", 1), ("gy", 2), ("gz", 3)), 1)
    return operate(field, padded, weights, total)


def assemble(gathered, leading):
    count_x = lax.axis_size("gx")
    count_y = lax.axis_size("gy")
    count_z = lax.axis_size("gz")
    rest = gathered.shape[1:]
    lead_shape = rest[:leading]
    brick = rest[leading:]
    grid = gathered.reshape((count_x, count_y, count_z) + rest)
    order = list(range(3, 3 + leading)) + [0, 3 + leading, 1, 4 + leading, 2, 5 + leading]
    grid = jnp.transpose(grid, order)
    return grid.reshape(lead_shape + (count_x * brick[0], count_y * brick[1], count_z * brick[2]))


def per_device(couplings, diagonal, right_side, guess):
    levels = hierarchy(couplings, diagonal)
    coarse_weights, coarse_total = levels[LEVELS - 1]
    whole_weights, whole_total = (
        lax.all_gather(coarse_weights[None], ("gx", "gy", "gz"), axis=0, tiled=True),
        lax.all_gather(coarse_total[None], ("gx", "gy", "gz"), axis=0, tiled=True),
    )
    whole_weights = assemble(whole_weights, 2)
    whole_total = assemble(whole_total, 1)

    def coarsest(rhs):
        whole_rhs = assemble(lax.all_gather(rhs[None], ("gx", "gy", "gz"), axis=0, tiled=True), 1)
        value = damping * whole_rhs / whole_total
        for step in range(COARSE_SWEEPS - 1):
            value = (
                value
                + damping
                * (whole_rhs - operate(value, pad_zero(value), whole_weights, whole_total))
                / whole_total
            )
        size_x, size_y, size_z = rhs.shape[1:]
        start_x = lax.axis_index("gx") * size_x
        start_y = lax.axis_index("gy") * size_y
        start_z = lax.axis_index("gz") * size_z
        return lax.dynamic_slice(value, (jnp.int32(0), start_x, start_y, start_z), rhs.shape)

    def cycle(level, field, rhs):
        if level == LEVELS - 1:
            return coarsest(rhs)
        weights, total = levels[level]
        if field is None:
            field = damping * rhs / total
            first = 1
        else:
            first = 0
        for step in range(first, SWEEPS):
            field = field + damping * (rhs - apply_brick(field, weights, total)) / total
        resid = rhs - apply_brick(field, weights, total)
        correction = cycle(level + 1, None, coarsen(resid))
        field = field + refine(correction)
        for step in range(SWEEPS):
            field = field + damping * (rhs - apply_brick(field, weights, total)) / total
        return field

    return cycle(0, guess, right_side)


def solution(mesh):
    return jax.shard_map(
        per_device,
        mesh=mesh,
        in_specs=(
            P(None, "gx", "gy", "gz"),
            P(None, "gx", "gy", "gz"),
            P(None, "gx", "gy", "gz"),
            P(None, "gx", "gy", "gz"),
        ),
        out_specs=P(None, "gx", "gy", "gz"),
        check_vma=False,
    )
```

profile of v0, /device:TPU:30, one launch (start us, length us, event | category | flops | bytes accessed | tf_op | source)
XLA Modules:
  0.0 472.0 jit_solution(790651737799890463)
XLA Ops:
  2.1 4.5 collective-permute-start
  11.8 4.2 collective-permute-done.3
  18.1 2.4 collective-permute-start.5
  21.8 3.8 collective-permute-done.5
  27.2 4.2 collective-permute-start.6
  32.8 4.2 collective-permute-done.7
  37.0 2.4 collective-permute-start.8
  40.8 4.2 collective-permute-done.9
  47.1 2.4 collective-permute-start.11
  50.8 3.8 collective-permute-done.11
  57.9 4.2 collective-permute-done.13
  62.1 2.4 collective-permute-start.14
  65.8 2.7 copy.419
  68.5 16.2 %reshape_reshape.3 = f32[3,6,4,2,4,2,64,2]{1,0,7,6,5,4,3,2:T(4,128)} reshape(f32[18,8,8,128]{0,3,2,1:T(8,128)} %copy.419) | data formatting | bytes 1179648 | tf_op jit(solution)/shard_map/reshape;reshape | solution.py:49
  84.8 10.0 %reduce_sum.141 = f32[3,6,4,4,64]{1,0,4,3,2:T(4,128)S(1)} reduce(f32[3,6,4,2,4,2,64,2]{1,0,7,6,5,4,3,2:T(4,128)} %reshape_reshape.3, f32[]{:T(128)} %constant.20.clone.1), dimensions={3,5,7}, to_apply=%region_3.0 | reduce | flops 129024 | bytes 663556 | tf_op jit(solution)/shard_map/reduce_sum | solution.py:50
  97.6 2.4 collective-permute-start.17
  100.1 7.7 %reshape.124 = f32[3,4,2,4,2,64,2]{6,5,4,3,2,1,0:T(8,128)} reshape(f32[3,8,8,128]{3,2,1,0:T(8,128)S(1)} %copy-done.2) | data formatting | bytes 196608 | tf_op jit(solution)/shard_map/reshape | solution.py:49
  107.8 3.3 reduce_sum.140
  111.3 7.7 %reshape.123 = f32[3,4,2,4,2,64,2]{6,5,4,3,2,1,0:T(8,128)} reshape(f32[3,8,8,128]{3,2,1,0:T(8,128)S(1)} %fusion.35) | data formatting | bytes 196608 | tf_op jit(solution)/shard_map/reshape | solution.py:49
  119.0 3.3 reduce_sum.139
  125.3 4.2 collective-permute-done.19
  129.5 4.5 collective-permute-start.20
  135.4 4.2 collective-permute-done.21
  141.7 2.4 collective-permute-start.23
  150.7 4.0 collective-permute-done.25
  158.1 4.2 collective-permute-done.27
  164.3 2.6 collective-permute-start.29
  174.1 36.7 %all-gather.2 = f32[96,6,16]{2,1,0:T(8,128)S(1)} all-gather(f32[3,6,16]{2,1,0:T(8,128)S(1)} %copy.426), channel_id=4, replica_groups=mesh['gx'=2,'gy'=4,'gz'=4] {'gx','gy','gz'}, dimensions={0}, use_global_device_ids=true | all-gather | bytes 38016 | tf_op jit(solution)/shard_map/all_gather | solution.py:91
  213.7 3.9 collective-permute-done.33
  217.8 4.3 collective-permute-start.34
  224.1 3.0 collective-permute-done.35
  230.8 4.2 collective-permute-done.37
  235.0 5.2 %collective-permute-start.38 = (f32[3,4,1,32]{3,2,1,0:T(1,128)S(1)}, f32[3,4,1,32]{3,2,1,0:T(1,128)S(1)}, u32[]{:S(2)}, u32[]{:S(2)}) collective-permute-start(f32[3,4,1,32]{3,2,1,0:T(1,128)S(1)} %get-tuple-element.94), channel_id=1, source_target_pairs={{4,0},{8,4},{12,8},{5,1},{9,5},{13,9},{6,2},{10,6},{14,10},{7,3},{... | collective-permute-start | bytes 4616 | tf_op jit(solution)/shard_map/ppermute | solution.py:22
  241.5 35.9 %all-gather.4 = f32[32,3,16]{2,1,0:T(4,128)S(1)} all-gather(f32[1,3,16]{2,1,0:T(4,128)S(1)} %add_bitcast_fusion), channel_id=3, replica_groups=mesh['gx'=2,'gy'=4,'gz'=4] {'gx','gy','gz'}, dimensions={0}, use_global_device_ids=true | all-gather | bytes 6336 | tf_op jit(solution)/shard_map/all_gather | solution.py:92
  279.5 2.4 collective-permute-start.41
  282.0 2.6 collective-permute-done.41
  285.0 38.4 %all-gather.3 = f32[32,3,16]{2,1,0:T(4,128)S(1)} all-gather(f32[1,3,16]{2,1,0:T(4,128)S(1)} %multiply_bitcast_fusion), channel_id=2, replica_groups=mesh['gx'=2,'gy'=4,'gz'=4] {'gx','gy','gz'}, dimensions={0}, use_global_device_ids=true | all-gather | bytes 6336 | tf_op jit(solution)/shard_map/all_gather | solution.py:98
  324.5 2.5 collective-permute-start.42
  328.3 4.2 collective-permute-done.43
  335.1 4.2 collective-permute-done.45
  341.3 2.4 collective-permute-start.47
  343.8 3.4 collective-permute-done.47
  350.2 4.2 collective-permute-done.49
  354.5 6.1 %collective-permute-start.50 = (f32[3,4,1,32]{3,2,1,0:T(1,128)S(1)}, f32[3,4,1,32]{3,2,1,0:T(1,128)S(1)}, u32[]{:S(2)}, u32[]{:S(2)}) collective-permute-start(f32[3,4,1,32]{3,2,1,0:T(1,128)S(1)} %get-tuple-element.90), channel_id=1, source_target_pairs={{4,0},{8,4},{12,8},{5,1},{9,5},{13,9},{6,2},{10,6},{14,10},{7,3},{... | collective-permute-start | bytes 4616 | tf_op jit(solution)/shard_map/ppermute | solution.py:22
  361.9 4.2 collective-permute-done.51
  368.1 2.4 collective-permute-start.53
  370.5 2.7 collective-permute-done.53
  376.9 4.2 collective-permute-done.55
  381.1 3.9 collective-permute-start.56
  386.4 4.2 collective-permute-done.57
  392.6 2.4 collective-permute-start.59
  395.0 3.2 collective-permute-done.59
  401.5 4.2 collective-permute-done.61
  409.0 4.2 collective-permute-done.63
  415.2 2.4 collective-permute-start.65
  417.6 3.2 collective-permute-done.65
  425.1 4.2 collective-permute-done.67
  432.7 4.2 collective-permute-done.69
  439.0 2.4 collective-permute-start.71
  442.7 3.8 collective-permute-done.71
  449.8 4.2 collective-permute-done.73
  457.3 4.2 collective-permute-done.75
  463.7 2.4 collective-permute-start.77
  467.4 3.8 collective-permute-done.77
  (234 shorter events, 114.4 us)
Async XLA Ops:
  0.8 5.8 %collective-permute-start.1 = (f32[3,1,8,128]{3,2,1,0:T(8,128)S(1)}, f32[3,1,8,128]{3,2,1,0:T(8,128)S(1)}, u32[]{:S(2)}, u32[]{:S(2)}) collective-permute-start(f32[3,1,8,128]{3,2,1,0:T(8,128)S(1)} %get-tuple-element.51), channel_id=1, source_target_pairs={{0,16},{1,17},{2,18},{3,19},{4,20},{5,21},{6,22},{7,23},{8,24},{9,... | collective-permute-start | bytes 36872 | tf_op jit(solution)/shard_map/ppermute | solution.py:19
  2.1 5.9 %collective-permute-start = (f32[3,1,8,128]{3,2,1,0:T(8,128)S(1)}, f32[3,1,8,128]{3,2,1,0:T(8,128)S(1)}, u32[]{:S(2)}, u32[]{:S(2)}) collective-permute-start(f32[3,1,8,128]{3,2,1,0:T(8,128)S(1)} %get-tuple-element.50), channel_id=1, source_target_pairs={{16,0},{17,1},{18,2},{19,3},{20,4},{21,5},{22,6},{23,7},{24,8},{25... | collective-permute-start | bytes 36872 | tf_op jit(solution)/shard_map/ppermute | solution.py:22
  8.1 3.8 collective-permute-start.2
  10.4 5.6 %collective-permute-start.3 = (f32[3,10,1,128]{3,2,1,0:T(1,128)S(1)}, f32[3,10,1,128]{3,2,1,0:T(1,128)S(1)}, u32[]{:S(2)}, u32[]{:S(2)}) collective-permute-start(f32[3,10,1,128]{3,2,1,0:T(1,128)S(1)} %get-tuple-element.40), channel_id=1, source_target_pairs={{0,4},{4,8},{8,12},{1,5},{5,9},{9,13},{2,6},{6,10},{10,14},{3,7},{... | collective-permute-start | bytes 46088 | tf_op jit(solution)/shard_map/ppermute | solution.py:19
  16.2 5.6 %collective-permute-start.4 = (f32[3,10,10,1]{3,2,1,0:T(8,128)S(1)}, f32[3,10,10,1]{3,2,1,0:T(8,128)S(1)}, u32[]{:S(2)}, u32[]{:S(2)}) collective-permute-start(f32[3,10,10,1]{3,2,1,0:T(8,128)S(1)} %get-tuple-element.27), channel_id=1, source_target_pairs={{1,0},{2,1},{3,2},{5,4},{6,5},{7,6},{9,8},{10,9},{11,10},{13,12},{... | collective-permute-start | bytes 3608 | tf_op jit(solution)/shard_map/ppermute | solution.py:22
  18.1 7.5 %collective-permute-start.5 = (f32[3,10,10,1]{3,2,1,0:T(8,128)S(1)}, f32[3,10,10,1]{3,2,1,0:T(8,128)S(1)}, u32[]{:S(2)}, u32[]{:S(2)}) collective-permute-start(f32[3,10,10,1]{3,2,1,0:T(8,128)S(1)} %get-tuple-element.28), channel_id=1, source_target_pairs={{0,1},{1,2},{2,3},{4,5},{5,6},{6,7},{8,9},{9,10},{10,11},{12,13},{... | collective-permute-start | bytes 3608 | tf_op jit(solution)/shard_map/ppermute | solution.py:19
  27.2 5.6 %collective-permute-start.6 = (f32[3,1,8,128]{3,2,1,0:T(8,128)S(1)}, f32[3,1,8,128]{3,2,1,0:T(8,128)S(1)}, u32[]{:S(2)}, u32[]{:S(2)}) collective-permute-start(f32[3,1,8,128]{3,2,1,0:T(8,128)S(1)} %get-tuple-element.49), channel_id=1, source_target_pairs={{16,0},{17,1},{18,2},{19,3},{20,4},{21,5},{22,6},{23,7},{24,8},{25... | collective-permute-start | bytes 36872 | tf_op jit(solution)/shard_map/ppermute | solution.py:22
  31.4 5.6 %collective-permute-start.7 = (f32[3,1,8,128]{3,2,1,0:T(8,128)S(1)}, f32[3,1,8,128]{3,2,1,0:T(8,128)S(1)}, u32[]{:S(2)}, u32[]{:S(2)}) collective-permute-start(f32[3,1,8,128]{3,2,1,0:T(8,128)S(1)} %get-tuple-element.48), channel_id=1, source_target_pairs={{0,16},{1,17},{2,18},{3,19},{4,20},{5,21},{6,22},{7,23},{8,24},{9,... | collective-permute-start | bytes 36872 | tf_op jit(solution)/shard_map/ppermute | solution.py:19
  37.0 3.8 collective-permute-start.8
  39.4 5.6 %collective-permute-start.9 = (f32[3,10,1,128]{3,2,1,0:T(1,128)S(1)}, f32[3,10,1,128]{3,2,1,0:T(1,128)S(1)}, u32[]{:S(2)}, u32[]{:S(2)}) collective-permute-start(f32[3,10,1,128]{3,2,1,0:T(1,128)S(1)} %get-tuple-element.38), channel_id=1, source_target_pairs={{0,4},{4,8},{8,12},{1,5},{5,9},{9,13},{2,6},{6,10},{10,14},{3,7},{... | collective-permute-start | bytes 46088 | tf_op jit(solution)/shard_map/ppermute | solution.py:19
  45.2 5.6 %collective-permute-start.10 = (f32[3,10,10,1]{3,2,1,0:T(8,128)S(1)}, f32[3,10,10,1]{3,2,1,0:T(8,128)S(1)}, u32[]{:S(2)}, u32[]{:S(2)}) collective-permute-start(f32[3,10,10,1]{3,2,1,0:T(8,128)S(1)} %get-tuple-element.25), channel_id=1, source_target_pairs={{1,0},{2,1},{3,2},{5,4},{6,5},{7,6},{9,8},{10,9},{11,10},{13,12},{... | collective-permute-start | bytes 3608 | tf_op jit(solution)/shard_map/ppermute | solution.py:22
  47.1 7.5 %collective-permute-start.11 = (f32[3,10,10,1]{3,2,1,0:T(8,128)S(1)}, f32[3,10,10,1]{3,2,1,0:T(8,128)S(1)}, u32[]{:S(2)}, u32[]{:S(2)}) collective-permute-start(f32[3,10,10,1]{3,2,1,0:T(8,128)S(1)} %get-tuple-element.26), channel_id=1, source_target_pairs={{0,1},{1,2},{2,3},{4,5},{5,6},{6,7},{8,9},{9,10},{10,11},{12,13},{... | collective-permute-start | bytes 3608 | tf_op jit(solution)/shard_map/ppermute | solution.py:19
  56.5 5.6 %collective-permute-start.13 = (f32[3,1,8,128]{3,2,1,0:T(8,128)S(1)}, f32[3,1,8,128]{3,2,1,0:T(8,128)S(1)}, u32[]{:S(2)}, u32[]{:S(2)}) collective-permute-start(f32[3,1,8,128]{3,2,1,0:T(8,128)S(1)} %get-tuple-element.46), channel_id=1, source_target_pairs={{0,16},{1,17},{2,18},{3,19},{4,20},{5,21},{6,22},{7,23},{8,24},{9,... | collective-permute-start | bytes 36872 | tf_op jit(solution)/shard_map/ppermute | solution.py:19
  62.1 33.4 %collective-permute-start.14 = (f32[3,10,1,128]{3,2,1,0:T(1,128)S(1)}, f32[3,10,1,128]{3,2,1,0:T(1,128)S(1)}, u32[]{:S(2)}, u32[]{:S(2)}) collective-permute-start(f32[3,10,1,128]{3,2,1,0:T(1,128)S(1)} %get-tuple-element.37), channel_id=1, source_target_pairs={{4,0},{8,4},{12,8},{5,1},{9,5},{13,9},{6,2},{10,6},{14,10},{7,3},{... | collective-permute-start | bytes 46088 | tf_op jit(solution)/shard_map/ppermute | solution.py:22
  64.5 31.0 %collective-permute-start.15 = (f32[3,10,1,128]{3,2,1,0:T(1,128)S(1)}, f32[3,10,1,128]{3,2,1,0:T(1,128)S(1)}, u32[]{:S(2)}, u32[]{:S(2)}) collective-permute-start(f32[3,10,1,128]{3,2,1,0:T(1,128)S(1)} %get-tuple-element.36), channel_id=1, source_target_pairs={{0,4},{4,8},{8,12},{1,5},{5,9},{9,13},{2,6},{6,10},{10,14},{3,7},{... | collective-permute-start | bytes 46088 | tf_op jit(solution)/shard_map/ppermute | solution.py:19
  95.7 15.4 %collective-permute-start.16 = (f32[3,10,10,1]{3,2,1,0:T(8,128)S(1)}, f32[3,10,10,1]{3,2,1,0:T(8,128)S(1)}, u32[]{:S(2)}, u32[]{:S(2)}) collective-permute-start(f32[3,10,10,1]{3,2,1,0:T(8,128)S(1)} %get-tuple-element.23), channel_id=1, source_target_pairs={{1,0},{2,1},{3,2},{5,4},{6,5},{7,6},{9,8},{10,9},{11,10},{13,12},{... | collective-permute-start | bytes 3608 | tf_op jit(solution)/shard_map/ppermute | solution.py:22
  97.6 13.5 %collective-permute-start.17 = (f32[3,10,10,1]{3,2,1,0:T(8,128)S(1)}, f32[3,10,10,1]{3,2,1,0:T(8,128)S(1)}, u32[]{:S(2)}, u32[]{:S(2)}) collective-permute-start(f32[3,10,10,1]{3,2,1,0:T(8,128)S(1)} %get-tuple-element.24), channel_id=1, source_target_pairs={{0,1},{1,2},{2,3},{4,5},{5,6},{6,7},{8,9},{9,10},{10,11},{12,13},{... | collective-permute-start | bytes 3608 | tf_op jit(solution)/shard_map/ppermute | solution.py:19
  124.0 5.5 %collective-permute-start.19 = (f32[3,1,4,64]{3,2,1,0:T(4,128)S(1)}, f32[3,1,4,64]{3,2,1,0:T(4,128)S(1)}, u32[]{:S(2)}, u32[]{:S(2)}) collective-permute-start(f32[3,1,4,64]{3,2,1,0:T(4,128)S(1)} %get-tuple-element.87), channel_id=1, source_target_pairs={{0,16},{1,17},{2,18},{3,19},{4,20},{5,21},{6,22},{7,23},{8,24},{9,... | collective-permute-start | bytes 9224 | tf_op jit(solution)/shard_map/ppermute | solution.py:19
  129.5 5.9 %collective-permute-start.20 = (f32[3,6,1,64]{3,2,1,0:T(1,128)S(1)}, f32[3,6,1,64]{3,2,1,0:T(1,128)S(1)}, u32[]{:S(2)}, u32[]{:S(2)}) collective-permute-start(f32[3,6,1,64]{3,2,1,0:T(1,128)S(1)} %get-tuple-element.69), channel_id=1, source_target_pairs={{4,0},{8,4},{12,8},{5,1},{9,5},{13,9},{6,2},{10,6},{14,10},{7,3},{... | collective-permute-start | bytes 13832 | tf_op jit(solution)/shard_map/ppermute | solution.py:22
  134.1 5.6 %collective-permute-start.21 = (f32[3,6,1,64]{3,2,1,0:T(1,128)S(1)}, f32[3,6,1,64]{3,2,1,0:T(1,128)S(1)}, u32[]{:S(2)}, u32[]{:S(2)}) collective-permute-start(f32[3,6,1,64]{3,2,1,0:T(1,128)S(1)} %get-tuple-element.68), channel_id=1, source_target_pairs={{0,4},{4,8},{8,12},{1,5},{5,9},{9,13},{2,6},{6,10},{10,14},{3,7},{... | collective-permute-start | bytes 13832 | tf_op jit(solution)/shard_map/ppermute | solution.py:19
  139.8 5.9 %collective-permute-start.22 = (f32[3,6,6,1]{3,2,1,0:T(8,128)S(1)}, f32[3,6,6,1]{3,2,1,0:T(8,128)S(1)}, u32[]{:S(2)}, u32[]{:S(2)}) collective-permute-start(f32[3,6,6,1]{3,2,1,0:T(8,128)S(1)} %get-tuple-element.60), channel_id=1, source_target_pairs={{1,0},{2,1},{3,2},{5,4},{6,5},{7,6},{9,8},{10,9},{11,10},{13,12},{... | collective-permute-start | bytes 1304 | tf_op jit(solution)/shard_map/ppermute | solution.py:22
  141.7 5.7 %collective-permute-start.23 = (f32[3,6,6,1]{3,2,1,0:T(8,128)S(1)}, f32[3,6,6,1]{3,2,1,0:T(8,128)S(1)}, u32[]{:S(2)}, u32[]{:S(2)}) collective-permute-start(f32[3,6,6,1]{3,2,1,0:T(8,128)S(1)} %get-tuple-element.61), channel_id=1, source_target_pairs={{0,1},{1,2},{2,3},{4,5},{5,6},{6,7},{8,9},{9,10},{10,11},{12,13},{... | collective-permute-start | bytes 1304 | tf_op jit(solution)/shard_map/ppermute | solution.py:19
  149.2 5.5 %collective-permute-start.25 = (f32[3,1,4,64]{3,2,1,0:T(4,128)S(1)}, f32[3,1,4,64]{3,2,1,0:T(4,128)S(1)}, u32[]{:S(2)}, u32[]{:S(2)}) collective-permute-start(f32[3,1,4,64]{3,2,1,0:T(4,128)S(1)} %get-tuple-element.85), channel_id=1, source_target_pairs={{0,16},{1,17},{2,18},{3,19},{4,20},{5,21},{6,22},{7,23},{8,24},{9,... | collective-permute-start | bytes 9224 | tf_op jit(solution)/shard_map/ppermute | solution.py:19
  156.7 5.6 %collective-permute-start.27 = (f32[3,6,1,64]{3,2,1,0:T(1,128)S(1)}, f32[3,6,1,64]{3,2,1,0:T(1,128)S(1)}, u32[]{:S(2)}, u32[]{:S(2)}) collective-permute-start(f32[3,6,1,64]{3,2,1,0:T(1,128)S(1)} %get-tuple-element.66), channel_id=1, source_target_pairs={{0,4},{4,8},{8,12},{1,5},{5,9},{9,13},{2,6},{6,10},{10,14},{3,7},{... | collective-permute-start | bytes 13832 | tf_op jit(solution)/shard_map/ppermute | solution.py:19
  162.3 6.3 %collective-permute-start.28 = (f32[3,6,6,1]{3,2,1,0:T(8,128)S(1)}, f32[3,6,6,1]{3,2,1,0:T(8,128)S(1)}, u32[]{:S(2)}, u32[]{:S(2)}) collective-permute-start(f32[3,6,6,1]{3,2,1,0:T(8,128)S(1)} %get-tuple-element.58), channel_id=1, source_target_pairs={{1,0},{2,1},{3,2},{5,4},{6,5},{7,6},{9,8},{10,9},{11,10},{13,12},{... | collective-permute-start | bytes 1304 | tf_op jit(solution)/shard_map/ppermute | solution.py:22
  164.3 5.7 %collective-permute-start.29 = (f32[3,6,6,1]{3,2,1,0:T(8,128)S(1)}, f32[3,6,6,1]{3,2,1,0:T(8,128)S(1)}, u32[]{:S(2)}, u32[]{:S(2)}) collective-permute-start(f32[3,6,6,1]{3,2,1,0:T(8,128)S(1)} %get-tuple-element.59), channel_id=1, source_target_pairs={{0,1},{1,2},{2,3},{4,5},{5,6},{6,7},{8,9},{9,10},{10,11},{12,13},{... | collective-permute-start | bytes 1304 | tf_op jit(solution)/shard_map/ppermute | solution.py:19
  171.1 39.7 %collective-permute-start.30 = (f32[3,1,2,32]{3,2,1,0:T(2,128)S(1)}, f32[3,1,2,32]{3,2,1,0:T(2,128)S(1)}, u32[]{:S(2)}, u32[]{:S(2)}) collective-permute-start(f32[3,1,2,32]{3,2,1,0:T(2,128)S(1)} %get-tuple-element.105), channel_id=1, source_target_pairs={{16,0},{17,1},{18,2},{19,3},{20,4},{21,5},{22,6},{23,7},{24,8},{25... | collective-permute-start | bytes 2312 | tf_op jit(solution)/shard_map/ppermute | solution.py:22
  172.8 38.0 %collective-permute-start.31 = (f32[3,1,2,32]{3,2,1,0:T(2,128)S(1)}, f32[3,1,2,32]{3,2,1,0:T(2,128)S(1)}, u32[]{:S(2)}, u32[]{:S(2)}) collective-permute-start(f32[3,1,2,32]{3,2,1,0:T(2,128)S(1)} %get-tuple-element.104), channel_id=1, source_target_pairs={{0,16},{1,17},{2,18},{3,19},{4,20},{5,21},{6,22},{7,23},{8,24},{9,... | collective-permute-start | bytes 2312 | tf_op jit(solution)/shard_map/ppermute | solution.py:19
  212.1 5.5 %collective-permute-start.33 = (f32[3,4,1,32]{3,2,1,0:T(1,128)S(1)}, f32[3,4,1,32]{3,2,1,0:T(1,128)S(1)}, u32[]{:S(2)}, u32[]{:S(2)}) collective-permute-start(f32[3,4,1,32]{3,2,1,0:T(1,128)S(1)} %get-tuple-element.95), channel_id=1, source_target_pairs={{0,4},{4,8},{8,12},{1,5},{5,9},{9,13},{2,6},{6,10},{10,14},{3,7},{... | collective-permute-start | bytes 4616 | tf_op jit(solution)/shard_map/ppermute | solution.py:19
  217.8 6.4 %collective-permute-start.34 = (f32[3,4,4,1]{3,2,1,0:T(4,128)S(1)}, f32[3,4,4,1]{3,2,1,0:T(4,128)S(1)}, u32[]{:S(2)}, u32[]{:S(2)}) collective-permute-start(f32[3,4,4,1]{3,2,1,0:T(4,128)S(1)} %get-tuple-element.82), channel_id=1, source_target_pairs={{1,0},{2,1},{3,2},{5,4},{6,5},{7,6},{9,8},{10,9},{11,10},{13,12},{... | collective-permute-start | bytes 584 | tf_op jit(solution)/shard_map/ppermute | solution.py:22
  222.0 5.1 %collective-permute-start.35 = (f32[3,4,4,1]{3,2,1,0:T(4,128)S(1)}, f32[3,4,4,1]{3,2,1,0:T(4,128)S(1)}, u32[]{:S(2)}, u32[]{:S(2)}) collective-permute-start(f32[3,4,4,1]{3,2,1,0:T(4,128)S(1)} %get-tuple-element.83), channel_id=1, source_target_pairs={{0,1},{1,2},{2,3},{4,5},{5,6},{6,7},{8,9},{9,10},{10,11},{12,13},{... | collective-permute-start | bytes 584 | tf_op jit(solution)/shard_map/ppermute | solution.py:19
  227.3 3.5 collective-permute-start.36
  229.5 5.5 %collective-permute-start.37 = (f32[3,1,2,32]{3,2,1,0:T(2,128)S(1)}, f32[3,1,2,32]{3,2,1,0:T(2,128)S(1)}, u32[]{:S(2)}, u32[]{:S(2)}) collective-permute-start(f32[3,1,2,32]{3,2,1,0:T(2,128)S(1)} %get-tuple-element.101), channel_id=1, source_target_pairs={{0,16},{1,17},{2,18},{3,19},{4,20},{5,21},{6,22},{7,23},{8,24},{9,... | collective-permute-start | bytes 2312 | tf_op jit(solution)/shard_map/ppermute | solution.py:19
  235.0 42.4 %collective-permute-start.38 = (f32[3,4,1,32]{3,2,1,0:T(1,128)S(1)}, f32[3,4,1,32]{3,2,1,0:T(1,128)S(1)}, u32[]{:S(2)}, u32[]{:S(2)}) collective-permute-start(f32[3,4,1,32]{3,2,1,0:T(1,128)S(1)} %get-tuple-element.94), channel_id=1, source_target_pairs={{4,0},{8,4},{12,8},{5,1},{9,5},{13,9},{6,2},{10,6},{14,10},{7,3},{... | collective-permute-start | bytes 4616 | tf_op jit(solution)/shard_map/ppermute | solution.py:22
  240.2 37.2 %collective-permute-start.39 = (f32[3,4,1,32]{3,2,1,0:T(1,128)S(1)}, f32[3,4,1,32]{3,2,1,0:T(1,128)S(1)}, u32[]{:S(2)}, u32[]{:S(2)}) collective-permute-start(f32[3,4,1,32]{3,2,1,0:T(1,128)S(1)} %get-tuple-element.93), channel_id=1, source_target_pairs={{0,4},{4,8},{8,12},{1,5},{5,9},{9,13},{2,6},{6,10},{10,14},{3,7},{... | collective-permute-start | bytes 4616 | tf_op jit(solution)/shard_map/ppermute | solution.py:19
  277.6 4.4 collective-permute-start.40
  279.5 5.1 %collective-permute-start.41 = (f32[3,4,4,1]{3,2,1,0:T(4,128)S(1)}, f32[3,4,4,1]{3,2,1,0:T(4,128)S(1)}, u32[]{:S(2)}, u32[]{:S(2)}) collective-permute-start(f32[3,4,4,1]{3,2,1,0:T(4,128)S(1)} %get-tuple-element.81), channel_id=1, source_target_pairs={{0,1},{1,2},{2,3},{4,5},{5,6},{6,7},{8,9},{9,10},{10,11},{12,13},{... | collective-permute-start | bytes 584 | tf_op jit(solution)/shard_map/ppermute | solution.py:19
  324.5 3.8 collective-permute-start.42
  327.0 5.5 %collective-permute-start.43 = (f32[3,1,2,32]{3,2,1,0:T(2,128)S(1)}, f32[3,1,2,32]{3,2,1,0:T(2,128)S(1)}, u32[]{:S(2)}, u32[]{:S(2)}) collective-permute-start(f32[3,1,2,32]{3,2,1,0:T(2,128)S(1)} %get-tuple-element.99), channel_id=1, source_target_pairs={{0,16},{1,17},{2,18},{3,19},{4,20},{5,21},{6,22},{7,23},{8,24},{9,... | collective-permute-start | bytes 2312 | tf_op jit(solution)/shard_map/ppermute | solution.py:19
  333.8 5.5 %collective-permute-start.45 = (f32[3,4,1,32]{3,2,1,0:T(1,128)S(1)}, f32[3,4,1,32]{3,2,1,0:T(1,128)S(1)}, u32[]{:S(2)}, u32[]{:S(2)}) collective-permute-start(f32[3,4,1,32]{3,2,1,0:T(1,128)S(1)} %get-tuple-element.91), channel_id=1, source_target_pairs={{0,4},{4,8},{8,12},{1,5},{5,9},{9,13},{2,6},{6,10},{10,14},{3,7},{... | collective-permute-start | bytes 4616 | tf_op jit(solution)/shard_map/ppermute | solution.py:19
  339.4 4.3 collective-permute-start.46
  341.3 5.8 %collective-permute-start.47 = (f32[3,4,4,1]{3,2,1,0:T(4,128)S(1)}, f32[3,4,4,1]{3,2,1,0:T(4,128)S(1)}, u32[]{:S(2)}, u32[]{:S(2)}) collective-permute-start(f32[3,4,4,1]{3,2,1,0:T(4,128)S(1)} %get-tuple-element.77), channel_id=1, source_target_pairs={{0,1},{1,2},{2,3},{4,5},{5,6},{6,7},{8,9},{9,10},{10,11},{12,13},{... | collective-permute-start | bytes 584 | tf_op jit(solution)/shard_map/ppermute | solution.py:19
  348.9 5.5 %collective-permute-start.49 = (f32[3,1,2,32]{3,2,1,0:T(2,128)S(1)}, f32[3,1,2,32]{3,2,1,0:T(2,128)S(1)}, u32[]{:S(2)}, u32[]{:S(2)}) collective-permute-start(f32[3,1,2,32]{3,2,1,0:T(2,128)S(1)} %get-tuple-element.97), channel_id=1, source_target_pairs={{0,16},{1,17},{2,18},{3,19},{4,20},{5,21},{6,22},{7,23},{8,24},{9,... | collective-permute-start | bytes 2312 | tf_op jit(solution)/shard_map/ppermute | solution.py:19
  354.5 7.4 %collective-permute-start.50 = (f32[3,4,1,32]{3,2,1,0:T(1,128)S(1)}, f32[3,4,1,32]{3,2,1,0:T(1,128)S(1)}, u32[]{:S(2)}, u32[]{:S(2)}) collective-permute-start(f32[3,4,1,32]{3,2,1,0:T(1,128)S(1)} %get-tuple-element.90), channel_id=1, source_target_pairs={{4,0},{8,4},{12,8},{5,1},{9,5},{13,9},{6,2},{10,6},{14,10},{7,3},{... | collective-permute-start | bytes 4616 | tf_op jit(solution)/shard_map/ppermute | solution.py:22
  360.5 5.5 %collective-permute-start.51 = (f32[3,4,1,32]{3,2,1,0:T(1,128)S(1)}, f32[3,4,1,32]{3,2,1,0:T(1,128)S(1)}, u32[]{:S(2)}, u32[]{:S(2)}) collective-permute-start(f32[3,4,1,32]{3,2,1,0:T(1,128)S(1)} %get-tuple-element.89), channel_id=1, source_target_pairs={{0,4},{4,8},{8,12},{1,5},{5,9},{9,13},{2,6},{6,10},{10,14},{3,7},{... | collective-permute-start | bytes 4616 | tf_op jit(solution)/shard_map/ppermute | solution.py:19
  366.2 4.3 collective-permute-start.52
  368.1 5.1 %collective-permute-start.53 = (f32[3,4,4,1]{3,2,1,0:T(4,128)S(1)}, f32[3,4,4,1]{3,2,1,0:T(4,128)S(1)}, u32[]{:S(2)}, u32[]{:S(2)}) collective-permute-start(f32[3,4,4,1]{3,2,1,0:T(4,128)S(1)} %get-tuple-element.75), channel_id=1, source_target_pairs={{0,1},{1,2},{2,3},{4,5},{5,6},{6,7},{8,9},{9,10},{10,11},{12,13},{... | collective-permute-start | bytes 584 | tf_op jit(solution)/shard_map/ppermute | solution.py:19
  375.5 5.5 %collective-permute-start.55 = (f32[3,1,4,64]{3,2,1,0:T(4,128)S(1)}, f32[3,1,4,64]{3,2,1,0:T(4,128)S(1)}, u32[]{:S(2)}, u32[]{:S(2)}) collective-permute-start(f32[3,1,4,64]{3,2,1,0:T(4,128)S(1)} %get-tuple-element.72), channel_id=1, source_target_pairs={{0,16},{1,17},{2,18},{3,19},{4,20},{5,21},{6,22},{7,23},{8,24},{9,... | collective-permute-start | bytes 9224 | tf_op jit(solution)/shard_map/ppermute | solution.py:19
  381.1 5.3 %collective-permute-start.56 = (f32[3,6,1,64]{3,2,1,0:T(1,128)S(1)}, f32[3,6,1,64]{3,2,1,0:T(1,128)S(1)}, u32[]{:S(2)}, u32[]{:S(2)}) collective-permute-start(f32[3,6,1,64]{3,2,1,0:T(1,128)S(1)} %get-tuple-element.65), channel_id=1, source_target_pairs={{4,0},{8,4},{12,8},{5,1},{9,5},{13,9},{6,2},{10,6},{14,10},{7,3},{... | collective-permute-start | bytes 13832 | tf_op jit(solution)/shard_map/ppermute | solution.py:22
  385.0 5.6 %collective-permute-start.57 = (f32[3,6,1,64]{3,2,1,0:T(1,128)S(1)}, f32[3,6,1,64]{3,2,1,0:T(1,128)S(1)}, u32[]{:S(2)}, u32[]{:S(2)}) collective-permute-start(f32[3,6,1,64]{3,2,1,0:T(1,128)S(1)} %get-tuple-element.64), channel_id=1, source_target_pairs={{0,4},{4,8},{8,12},{1,5},{5,9},{9,13},{2,6},{6,10},{10,14},{3,7},{... | collective-permute-start | bytes 13832 | tf_op jit(solution)/shard_map/ppermute | solution.py:19
  390.7 4.3 collective-permute-start.58
  392.6 5.7 %collective-permute-start.59 = (f32[3,6,6,1]{3,2,1,0:T(8,128)S(1)}, f32[3,6,6,1]{3,2,1,0:T(8,128)S(1)}, u32[]{:S(2)}, u32[]{:S(2)}) collective-permute-start(f32[3,6,6,1]{3,2,1,0:T(8,128)S(1)} %get-tuple-element.57), channel_id=1, source_target_pairs={{0,1},{1,2},{2,3},{4,5},{5,6},{6,7},{8,9},{9,10},{10,11},{12,13},{... | collective-permute-start | bytes 1304 | tf_op jit(solution)/shard_map/ppermute | solution.py:19
  400.1 5.5 %collective-permute-start.61 = (f32[3,1,4,64]{3,2,1,0:T(4,128)S(1)}, f32[3,1,4,64]{3,2,1,0:T(4,128)S(1)}, u32[]{:S(2)}, u32[]{:S(2)}) collective-permute-start(f32[3,1,4,64]{3,2,1,0:T(4,128)S(1)} %get-tuple-element.70), channel_id=1, source_target_pairs={{0,16},{1,17},{2,18},{3,19},{4,20},{5,21},{6,22},{7,23},{8,24},{9,... | collective-permute-start | bytes 9224 | tf_op jit(solution)/shard_map/ppermute | solution.py:19
  407.6 5.6 %collective-permute-start.63 = (f32[3,6,1,64]{3,2,1,0:T(1,128)S(1)}, f32[3,6,1,64]{3,2,1,0:T(1,128)S(1)}, u32[]{:S(2)}, u32[]{:S(2)}) collective-permute-start(f32[3,6,1,64]{3,2,1,0:T(1,128)S(1)} %get-tuple-element.62), channel_id=1, source_target_pairs={{0,4},{4,8},{8,12},{1,5},{5,9},{9,13},{2,6},{6,10},{10,14},{3,7},{... | collective-permute-start | bytes 13832 | tf_op jit(solution)/shard_map/ppermute | solution.py:19
  413.3 4.3 collective-permute-start.64
  415.2 5.7 %collective-permute-start.65 = (f32[3,6,6,1]{3,2,1,0:T(8,128)S(1)}, f32[3,6,6,1]{3,2,1,0:T(8,128)S(1)}, u32[]{:S(2)}, u32[]{:S(2)}) collective-permute-start(f32[3,6,6,1]{3,2,1,0:T(8,128)S(1)} %get-tuple-element.55), channel_id=1, source_target_pairs={{0,1},{1,2},{2,3},{4,5},{5,6},{6,7},{8,9},{9,10},{10,11},{12,13},{... | collective-permute-start | bytes 1304 | tf_op jit(solution)/shard_map/ppermute | solution.py:19
  423.7 5.6 %collective-permute-start.67 = (f32[3,1,8,128]{3,2,1,0:T(8,128)S(1)}, f32[3,1,8,128]{3,2,1,0:T(8,128)S(1)}, u32[]{:S(2)}, u32[]{:S(2)}) collective-permute-start(f32[3,1,8,128]{3,2,1,0:T(8,128)S(1)} %get-tuple-element.44), channel_id=1, source_target_pairs={{0,16},{1,17},{2,18},{3,19},{4,20},{5,21},{6,22},{7,23},{8,24},{9,... | collective-permute-start | bytes 36872 | tf_op jit(solution)/shard_map/ppermute | solution.py:19
  431.2 5.6 %collective-permute-start.69 = (f32[3,10,1,128]{3,2,1,0:T(1,128)S(1)}, f32[3,10,1,128]{3,2,1,0:T(1,128)S(1)}, u32[]{:S(2)}, u32[]{:S(2)}) collective-permute-start(f32[3,10,1,128]{3,2,1,0:T(1,128)S(1)} %get-tuple-element.34), channel_id=1, source_target_pairs={{0,4},{4,8},{8,12},{1,5},{5,9},{9,13},{2,6},{6,10},{10,14},{3,7},{... | collective-permute-start | bytes 46088 | tf_op jit(solution)/shard_map/ppermute | solution.py:19
  437.1 5.6 %collective-permute-start.70 = (f32[3,10,10,1]{3,2,1,0:T(8,128)S(1)}, f32[3,10,10,1]{3,2,1,0:T(8,128)S(1)}, u32[]{:S(2)}, u32[]{:S(2)}) collective-permute-start(f32[3,10,10,1]{3,2,1,0:T(8,128)S(1)} %get-tuple-element.21), channel_id=1, source_target_pairs={{1,0},{2,1},{3,2},{5,4},{6,5},{7,6},{9,8},{10,9},{11,10},{13,12},{... | collective-permute-start | bytes 3608 | tf_op jit(solution)/shard_map/ppermute | solution.py:22
  439.0 7.5 %collective-permute-start.71 = (f32[3,10,10,1]{3,2,1,0:T(8,128)S(1)}, f32[3,10,10,1]{3,2,1,0:T(8,128)S(1)}, u32[]{:S(2)}, u32[]{:S(2)}) collective-permute-start(f32[3,10,10,1]{3,2,1,0:T(8,128)S(1)} %get-tuple-element.22), channel_id=1, source_target_pairs={{0,1},{1,2},{2,3},{4,5},{5,6},{6,7},{8,9},{9,10},{10,11},{12,13},{... | collective-permute-start | bytes 3608 | tf_op jit(solution)/shard_map/ppermute | solution.py:19
  448.4 5.6 %collective-permute-start.73 = (f32[3,1,8,128]{3,2,1,0:T(8,128)S(1)}, f32[3,1,8,128]{3,2,1,0:T(8,128)S(1)}, u32[]{:S(2)}, u32[]{:S(2)}) collective-permute-start(f32[3,1,8,128]{3,2,1,0:T(8,128)S(1)} %get-tuple-element.42), channel_id=1, source_target_pairs={{0,16},{1,17},{2,18},{3,19},{4,20},{5,21},{6,22},{7,23},{8,24},{9,... | collective-permute-start | bytes 36872 | tf_op jit(solution)/shard_map/ppermute | solution.py:19
  455.9 5.6 %collective-permute-start.75 = (f32[3,10,1,128]{3,2,1,0:T(1,128)S(1)}, f32[3,10,1,128]{3,2,1,0:T(1,128)S(1)}, u32[]{:S(2)}, u32[]{:S(2)}) collective-permute-start(f32[3,10,1,128]{3,2,1,0:T(1,128)S(1)} %get-tuple-element.32), channel_id=1, source_target_pairs={{0,4},{4,8},{8,12},{1,5},{5,9},{9,13},{2,6},{6,10},{10,14},{3,7},{... | collective-permute-start | bytes 46088 | tf_op jit(solution)/shard_map/ppermute | solution.py:19
  461.7 5.6 %collective-permute-start.76 = (f32[3,10,10,1]{3,2,1,0:T(8,128)S(1)}, f32[3,10,10,1]{3,2,1,0:T(8,128)S(1)}, u32[]{:S(2)}, u32[]{:S(2)}) collective-permute-start(f32[3,10,10,1]{3,2,1,0:T(8,128)S(1)} %get-tuple-element.19), channel_id=1, source_target_pairs={{1,0},{2,1},{3,2},{5,4},{6,5},{7,6},{9,8},{10,9},{11,10},{13,12},{... | collective-permute-start | bytes 3608 | tf_op jit(solution)/shard_map/ppermute | solution.py:22
  463.7 7.5 %collective-permute-start.77 = (f32[3,10,10,1]{3,2,1,0:T(8,128)S(1)}, f32[3,10,10,1]{3,2,1,0:T(8,128)S(1)}, u32[]{:S(2)}, u32[]{:S(2)}) collective-permute-start(f32[3,10,10,1]{3,2,1,0:T(8,128)S(1)} %get-tuple-element.20), channel_id=1, source_target_pairs={{0,1},{1,2},{2,3},{4,5},{5,6},{6,7},{8,9},{9,10},{10,11},{12,13},{... | collective-permute-start | bytes 3608 | tf_op jit(solution)/shard_map/ppermute | solution.py:19
  (17 other events, 167.6 us)
where the time goes:
time: 475 us; the launch traced here: 472 us
  starting transfers between devices  157 us (33%)
  waiting for transfers between devices  134 us (28%)
  blocking collectives  111 us (23%)
  local copies, waits for them, and re-layouts  43.3 us (9%)
  other arithmetic  25.2 us (5%)
    ppermute x39, waiting for transfers between devices, padded_2(): lax.ppermute(lax.slice_in_dim(block, block.shape[dim] - width, None, axis...  128 us
    ppermute x39, starting transfers between devices, padded_2(): lax.ppermute(lax.slice_in_dim(block, 0, width, axis=dim), axis, backward)  92.5 us
    ppermute x39, starting transfers between devices, padded_2(): lax.ppermute(lax.slice_in_dim(block, block.shape[dim] - width, None, axis...  64.6 us
    all_gather x1, blocking collectives, coarsest(): lax.all_gather(rhs[None], ('gx', 'gy', 'gz'), axis=0, tiled=True)  38.4 us
    all_gather x1, blocking collectives, per_device(): lax.all_gather(coarse_weights[None], ('gx', 'gy', 'gz'), axis=0, tiled=True)  36.7 us
    all_gather x1, blocking collectives, per_device(): lax.all_gather(coarse_total[None], ('gx', 'gy', 'gz'), axis=0, tiled=True)  35.9 us
    reduce_sum x11, other arithmetic, coarsen(): return jnp.mean(blocks, axis=(count - 2, count, count + 2))  18.3 us
    another operation x1, local copies, waits for them, and re-layouts, coarsen(): array.reshape(shape[:-3] + (shape[-3] // 2, 2, shape[-2] // 2, 2, shape[-...  16.2 us
  transfers between devices with their start and end apart: 78, of which 50 were waited for; matrix products, arithmetic and copies ran while one was open for 10% of the time, Pallas kernels for 0%

commit v1 on v0

v1 whole, which is shorter than its diff:
```python
import functools

import jax
import jax.numpy as jnp
from jax import lax
from jax.experimental import pallas as pl
from jax.experimental.pallas import tpu as pltpu
from jax.sharding import PartitionSpec as P

SWEEPS = 2
COARSE_SWEEPS = 8
DAMP = 0.8
EQ = 3
MESH = pl.DeviceIdType.MESH
HIGH = lax.Precision.HIGHEST


def roll(value, shift, axis):
    size = value.shape[axis]
    shift = shift % size
    return value if shift == 0 else pltpu.roll(value, shift, axis)


def iota(shape, axis):
    return lax.broadcasted_iota(jnp.int32, shape, axis)


def kernel(
    dims, cores, w_ref, d_ref, b_ref, g_ref, out_ref,
    field, halo_x, halo_y, pack_s, pack_r, tot0, c0, w1, tot1, c1, b1,
    wsend, wall, bsend, ball, e2,
    s_sem, r_sem, ws_sem, wr_sem, bs_sem, br_sem, l_sem,
):
    ngx, ngy, ngz = dims
    nx, ny, nz = g_ref.shape[1:]
    qx, qy, qz = nx // 4, ny // 4, nz // 4
    rows = ngx * ngy
    nX = ngz // cores
    gx, gy, gz = lax.axis_index("gx"), lax.axis_index("gy"), lax.axis_index("gz")
    X, core = gz // cores, gz % cores
    row = gx * ngy + gy
    axes = (("gx", gx, ngx), ("gy", gy, ngy), ("gz", gz, ngz))

    def device(name, index):
        here = {"gx": gx, "gy": gy, "gz": gz}
        here[name] = index
        return (here["gx"], here["gy"], here["gz"])

    barrier = pltpu.get_barrier_semaphore()
    for name, index, count in axes:
        for step in range(1, count):
            pl.semaphore_signal(
                barrier, inc=1, device_id=device(name, (index + step) % count), device_id_type=MESH
            )

    rounds = field.shape[0]
    for name, index, count in axes:
        for side in range(2):
            @pl.when(index == (0 if side == 0 else count - 1))
            def _():
                for r in range(rounds):
                    if name == "gx":
                        halo_x[r, side] = jnp.zeros(halo_x.shape[2:], jnp.float32)
                    elif name == "gy":
                        lo = 0 if side == 0 else ny // 2
                        halo_y[r, :, :, lo : lo + ny // 2] = jnp.zeros(
                            (EQ, nx, ny // 2, nz), jnp.float32
                        )
                    else:
                        pack_r[r, side] = jnp.zeros(pack_r.shape[2:], jnp.float32)

    pl.semaphore_wait(barrier, ngx + ngy + ngz - 3)

    lane2 = iota((ny, nz), 1)

    def copies(r, n, s):
        src = g_ref if r == 0 else field.at[r]
        made = []
        for side in range(2):
            other = 1 - side
            for place, (name, index, count) in enumerate(axes):
                if name == "gx":
                    a = src.at[:, 0 if side == 0 else n - 1]
                    z = halo_x.at[r, other]
                elif name == "gy":
                    a = src.at[:, 0:n, pl.ds(0 if side == 0 else ny - s, s)]
                    z = halo_y.at[r, :, 0:n, pl.ds(ny - s if side == 0 else 0, s)]
                else:
                    a = pack_s.at[r, side]
                    z = pack_r.at[r, other]
                target = index - 1 if side == 0 else index + 1
                has_target = index > 0 if side == 0 else index < count - 1
                has_source = index < count - 1 if side == 0 else index > 0
                slot = 2 * place + side
                made.append((
                    pltpu.make_async_remote_copy(
                        src_ref=a, dst_ref=z,
                        send_sem=s_sem.at[r, slot], recv_sem=r_sem.at[r, slot],
                        device_id=device(name, jnp.clip(target, 0, count - 1)),
                        device_id_type=MESH,
                    ),
                    has_target, has_source,
                ))
        return made

    def send(r, value, n, s):
        low = jnp.zeros((ny, nz), jnp.float32)
        high = jnp.zeros((ny, nz), jnp.float32)
        for e in range(EQ):
            if r > 0:
                field[r, e, 0:n] = value[e]
            for i in range(n):
                here = lane2 == e * n + i
                low = jnp.where(here, jnp.broadcast_to(value[e][i, :, 0:1], (ny, nz)), low)
                high = jnp.where(here, jnp.broadcast_to(value[e][i, :, nz - 1 : nz], (ny, nz)), high)
        pack_s[r, 0] = low
        pack_s[r, 1] = high
        for copy, has_target, _ in copies(r, n, s):
            @pl.when(has_target)
            def _():
                copy.start()

    def receive(r, n, s):
        for copy, _, has_source in copies(r, n, s):
            @pl.when(has_source)
            def _():
                copy.wait_recv()

    def near_sum(r, value, e, n, s, weight):
        v = value[e]
        shape = (n, ny, nz)
        y, z = iota(shape, 1), iota(shape, 2)
        hy = halo_y[r, e, 0:n]
        low = pack_r[r, 0]
        high = pack_r[r, 1]
        zl = jnp.stack([jnp.broadcast_to(low[:, e * n + i : e * n + i + 1], (ny, nz)) for i in range(n)])
        zh = jnp.stack([jnp.broadcast_to(high[:, e * n + i : e * n + i + 1], (ny, nz)) for i in range(n)])
        near = [
            jnp.concatenate([v[1:], halo_x[r, 1, e][None]], axis=0),
            jnp.concatenate([halo_x[r, 0, e][None], v[:-1]], axis=0),
            jnp.where(y >= ny - s, hy, roll(v, -s, 1)),
            jnp.where(y < s, hy, roll(v, s, 1)),
            jnp.where(z >= nz - s, zh, roll(v, -s, 2)),
            jnp.where(z < s, zl, roll(v, s, 2)),
        ]
        total = weight(e, 0) * near[0]
        for k in range(1, 6):
            total = total + weight(e, k) * near[k]
        return total

    def coarsen(a, s):
        n = a.shape[0]
        a = jnp.stack([a[2 * i] + a[2 * i + 1] for i in range(n // 2)])
        y, z = iota(a.shape, 1), iota(a.shape, 2)
        a = a + jnp.where((y // s) % 2 == 0, roll(a, -s, 1), roll(a, s, 1))
        a = a + jnp.where((z // s) % 2 == 0, roll(a, -s, 2), roll(a, s, 2))
        return a * 0.125

    def spread(a):
        return jnp.stack([a[i // 2] for i in range(2 * a.shape[0])])

    def weight0(e, k):
        return w_ref[6 * e + k]

    def weight1(e, k):
        return w1[6 * e + k]

    source = iota((nz, nz), 0)
    target = iota((nz, nz), 1)
    squeeze = jnp.where(source == 4 * (target % qz), 1.0, 0.0).astype(jnp.float32)

    def to_rows(a):
        m = a.shape[0]
        c = jnp.dot(a.reshape(m * qx * ny, nz), squeeze, precision=HIGH,
                    preferred_element_type=jnp.float32).reshape(m, qx, ny, nz)
        shape = (m, ny, nz)
        lane = iota(shape, 2)
        got = jnp.zeros(shape, jnp.float32)
        for x in range(qx):
            for y in range(qy):
                part = roll(c[:, x], -4 * y, 1)
                got = jnp.where(lane // qz == x * qy + y, part, got)
        return got

    def own(small, whole, sem):
        return pltpu.make_async_copy(
            small.at[:, pl.ds(0, 1)], whole.at[X, core, :, pl.ds(row, 1)], sem
        )

    def stage(number, small, whole, ss, rs):
        made = []
        if number == 0:
            for step in range(1, ngy):
                made.append((small.at[:, pl.ds(0, 1)], whole.at[X, core, :, pl.ds(row, 1)],
                             step, device("gy", (gy + step) % ngy)))
        elif number == 1:
            block = whole.at[X, core, :, pl.ds(gx * ngy, ngy)]
            for step in range(1, ngx):
                made.append((block, block, step, device("gx", (gx + step) % ngx)))
        elif number == 2:
            block = whole.at[X, core]
            for step in range(1, nX):
                made.append((block, block, step, device("gz", ((X + step) % nX) * cores + core)))
        else:
            block = whole.at[:, core]
            for step in range(1, cores):
                made.append((block, block, step, device("gz", X * cores + (core + step) % cores)))
        return [
            pltpu.make_async_remote_copy(
                src_ref=a, dst_ref=z, send_sem=ss.at[number, step], recv_sem=rs.at[number, step],
                device_id=where, device_id_type=MESH,
            )
            for a, z, step, where in made
        ]

    wargs = (wsend, wall, ws_sem, wr_sem)
    bargs = (bsend, ball, bs_sem, br_sem)

    def start(number, args):
        for copy in stage(number, *args):
            copy.start()

    def finish(number, args):
        for copy in stage(number, *args):
            copy.wait_recv()

    v = [g_ref[e] for e in range(EQ)]
    send(0, v, nx, 1)
    for e in range(EQ):
        total = d_ref[e]
        for k in range(6):
            total = total + w_ref[6 * e + k]
        tot0[e] = total
        c0[e] = DAMP / total
        total = coarsen(d_ref[e], 1)
        wsend_d = coarsen(total, 2)
        for k in range(6):
            w = 0.25 * coarsen(w_ref[6 * e + k], 1)
            w1[6 * e + k] = w
            total = total + w
            wsend[6 * e + k] = to_rows((0.25 * coarsen(w, 2))[None])[0]
        wsend[6 * EQ + e] = to_rows(wsend_d[None])[0]
        tot1[e] = total
        c1[e] = DAMP / total
    own(wsend, wall, l_sem.at[0]).start()
    start(0, wargs)

    def smooth0(r, v):
        return [
            (1.0 - DAMP) * v[e] + c0[e] * (b_ref[e] + near_sum(r, v, e, nx, 1, weight0))
            for e in range(EQ)
        ]

    def smooth1(r, v):
        return [
            (1.0 - DAMP) * v[e] + c1[e] * (b1[e] + near_sum(r, v, e, nx // 2, 2, weight1))
            for e in range(EQ)
        ]

    receive(0, nx, 1)
    v = smooth0(0, v)
    send(1, v, nx, 1)
    receive(1, nx, 1)
    v = smooth0(1, v)
    send(2, v, nx, 1)
    own(wsend, wall, l_sem.at[0]).wait()
    finish(0, wargs)
    start(1, wargs)
    receive(2, nx, 1)
    u = []
    for e in range(EQ):
        rest = b_ref[e] - tot0[e] * v[e] + near_sum(2, v, e, nx, 1, weight0)
        b = coarsen(rest, 1)
        b1[e] = b
        u.append(c1[e] * b)
    half = nx // 2
    send(3, u, half, 2)
    finish(1, wargs)
    start(2, wargs)
    receive(3, half, 2)
    u = smooth1(3, u)
    send(4, u, half, 2)
    finish(2, wargs)
    start(3, wargs)
    receive(4, half, 2)
    for e in range(EQ):
        rest = b1[e] - tot1[e] * u[e] + near_sum(4, u, e, half, 2, weight1)
        bsend[e] = to_rows(coarsen(rest, 2)[None])[0]
    own(bsend, ball, l_sem.at[1]).start()
    start(0, bargs)
    finish(3, wargs)

    shape = (ngz, rows, nz)
    r_i, l_i = iota(shape, 1), iota(shape, 2)
    g_i = iota(shape, 0)
    zi, yi, xi = l_i % qz, (l_i // qz) % qy, l_i // (qz * qy)
    gyi, gxi = r_i % ngy, r_i // ngy
    inside = [
        ~((xi == qx - 1) & (gxi == ngx - 1)), ~((xi == 0) & (gxi == 0)),
        ~((yi == qy - 1) & (gyi == ngy - 1)), ~((yi == 0) & (gyi == 0)),
        ~((zi == qz - 1) & (g_i == ngz - 1)), ~((zi == 0) & (g_i == 0)),
    ]

    def whole(ref, index):
        return ref[:, :, index].reshape(shape)

    def next_of(v):
        return jnp.concatenate([v[1:], v[:1]], axis=0)

    def prev_of(v):
        return jnp.concatenate([v[-1:], v[:-1]], axis=0)

    def near2(v):
        sy, sx = qz, qz * qy
        return [
            jnp.where(xi == qx - 1, roll(roll(v, (qx - 1) * sx, 2), -ngy, 1), roll(v, -sx, 2)),
            jnp.where(xi == 0, roll(roll(v, -(qx - 1) * sx, 2), ngy, 1), roll(v, sx, 2)),
            jnp.where(yi == qy - 1, roll(roll(v, (qy - 1) * sy, 2), -1, 1), roll(v, -sy, 2)),
            jnp.where(yi == 0, roll(roll(v, -(qy - 1) * sy, 2), 1, 1), roll(v, sy, 2)),
            jnp.where(zi == qz - 1, roll(next_of(v), qz - 1, 2), roll(v, -1, 2)),
            jnp.where(zi == 0, roll(prev_of(v), -(qz - 1), 2), roll(v, 1, 2)),
        ]

    def dot_near(weights, near):
        total = weights[0] * near[0]
        for k in range(1, 6):
            total = total + weights[k] * near[k]
        return total

    def pair(a):
        sy, sx = qz, qz * qy
        a = a + jnp.where(xi % 2 == 0, roll(a, -sx, 2), roll(a, sx, 2))
        a = a + jnp.where(yi % 2 == 0, roll(a, -sy, 2), roll(a, sy, 2))
        a = a + jnp.where(zi % 2 == 0, roll(a, -1, 2), roll(a, 1, 2))
        return a * 0.125

    groups = qx * qy
    tiles = ngz // groups
    shape3 = (tiles, rows, nz)
    r3, l3, t3 = iota(shape3, 1), iota(shape3, 2), iota(shape3, 0)
    inside3 = [
        r3 // ngy < ngx - 1, r3 // ngy > 0, r3 % ngy < ngy - 1, r3 % ngy > 0,
        ~((l3 >= nz - 2) & (t3 == tiles - 1)), ~((l3 < 2) & (t3 == 0)),
    ]

    def join(a):
        a = a.reshape(tiles, groups, rows, nz)
        got = a[:, 0]
        for j in range(1, groups):
            got = jnp.where(l3 // qz == j, a[:, j], got)
        return got

    def part(a):
        parts = []
        for j in range(groups):
            mine = jnp.where(l3 // qz == j, a, 0.0)
            size = qz
            while size < nz:
                mine = mine + roll(mine, size, 2)
                size *= 2
            parts.append(mine)
        return jnp.stack(parts, axis=1).reshape(shape)

    def near3(v):
        if tiles == 1:
            up, down = roll(v, -2, 2), roll(v, 2, 2)
        else:
            up = jnp.where(l3 >= nz - 2, roll(next_of(v), -2, 2), roll(v, -2, 2))
            down = jnp.where(l3 < 2, roll(prev_of(v), 2, 2), roll(v, 2, 2))
        return [roll(v, -ngy, 1), roll(v, ngy, 1), roll(v, -1, 1), roll(v, 1, 1), up, down]

    w2, t2, w3, t3s = [], [], [], []
    for e in range(EQ):
        plain = [whole(wall, 6 * e + k) for k in range(6)]
        d2 = whole(wall, 6 * EQ + e)
        total = d2
        for k in range(6):
            total = total + plain[k]
        t2.append(total)
        w2.append([jnp.where(inside[k], plain[k], 0.0) for k in range(6)])
        plain3 = [0.25 * join(pair(plain[k])) for k in range(6)]
        total = join(pair(d2))
        for k in range(6):
            total = total + plain3[k]
        t3s.append(total)
        w3.append([jnp.where(inside3[k], plain3[k], 0.0) for k in range(6)])
    c2 = [DAMP / t for t in t2]
    c3 = [DAMP / t for t in t3s]

    own(bsend, ball, l_sem.at[1]).wait()
    finish(0, bargs)
    for number in range(1, 4):
        start(number, bargs)
        finish(number, bargs)

    keep = 1.0 - DAMP
    for e in range(EQ):
        rhs = whole(ball, e)
        v2 = c2[e] * rhs
        for step in range(SWEEPS - 1):
            v2 = keep * v2 + c2[e] * (rhs + dot_near(w2[e], near2(v2)))
        rest = rhs - t2[e] * v2 + dot_near(w2[e], near2(v2))
        rhs3 = join(pair(rest))
        v3 = c3[e] * rhs3
        for step in range(COARSE_SWEEPS - 1):
            v3 = keep * v3 + c3[e] * (rhs3 + dot_near(w3[e], near3(v3)))
        v2 = v2 + part(v3)
        for step in range(SWEEPS):
            v2 = keep * v2 + c2[e] * (rhs + dot_near(w2[e], near2(v2)))
        e2[e] = v2

    wide = groups * nz
    source = iota((nz, wide), 0)
    target = iota((nz, wide), 1)
    widen = jnp.where(source == (target // nz) * qz + (target % nz) // 4, 1.0, 0.0).astype(jnp.float32)
    back = jnp.concatenate(
        [jnp.broadcast_to(e2[e, gz, pl.ds(row, 1), :], (ny, nz)) for e in range(EQ)], axis=0
    )
    back = jnp.dot(back, widen, precision=HIGH, preferred_element_type=jnp.float32)
    ysel = iota((ny, nz), 0) // 4
    for e in range(EQ):
        planes = []
        for x in range(qx):
            got = back[e * ny : (e + 1) * ny, (x * qy) * nz : (x * qy + 1) * nz]
            for y in range(1, qy):
                col = (x * qy + y) * nz
                got = jnp.where(ysel == y, back[e * ny : (e + 1) * ny, col : col + nz], got)
            planes.append(got)
        u[e] = u[e] + spread(jnp.stack(planes))
    send(5, u, half, 2)
    receive(5, half, 2)
    u = smooth1(5, u)
    send(6, u, half, 2)
    receive(6, half, 2)
    u = smooth1(6, u)
    v = [field[2, e] + spread(u[e]) for e in range(EQ)]
    send(7, v, nx, 1)
    receive(7, nx, 1)
    v = smooth0(7, v)
    send(8, v, nx, 1)
    receive(8, nx, 1)
    v = smooth0(8, v)
    for e in range(EQ):
        out_ref[e] = v[e]

    for r in range(rounds):
        n, s = (half, 2) if 3 <= r <= 6 else (nx, 1)
        for copy, has_target, _ in copies(r, n, s):
            @pl.when(has_target)
            def _():
                copy.wait_send()
    for args in (wargs, bargs):
        for number in range(4):
            for copy in stage(number, *args):
                copy.wait_send()


def per_device(dims, cores, couplings, diagonal, right_side, guess):
    ngx, ngy, ngz = dims
    brick = guess.shape[1:]
    nx, ny, nz = brick
    half = nx // 2
    rows = ngx * ngy
    nX = ngz // cores
    rounds = 9
    peers = max(ngx, ngy, nX, cores)
    f32 = jnp.float32
    vmem = pltpu.VMEM
    dma = pltpu.SemaphoreType.DMA
    return pl.pallas_call(
        functools.partial(kernel, dims, cores),
        out_shape=jax.ShapeDtypeStruct(guess.shape, f32),
        in_specs=[pl.BlockSpec(memory_space=vmem)] * 4,
        out_specs=pl.BlockSpec(memory_space=vmem),
        scratch_shapes=[
            vmem((rounds, EQ) + brick, f32),
            vmem((rounds, 2, EQ, ny, nz), f32),
            vmem((rounds, EQ) + brick, f32),
            vmem((rounds, 2, ny, nz), f32),
            vmem((rounds, 2, ny, nz), f32),
            vmem((EQ,) + brick, f32),
            vmem((EQ,) + brick, f32),
            vmem((6 * EQ, half, ny, nz), f32),
            vmem((EQ, half, ny, nz), f32),
            vmem((EQ, half, ny, nz), f32),
            vmem((EQ, half, ny, nz), f32),
            vmem((7 * EQ, ny, nz), f32),
            vmem((nX, cores, 7 * EQ, rows, nz), f32),
            vmem((EQ, ny, nz), f32),
            vmem((nX, cores, EQ, rows, nz), f32),
            vmem((EQ, ngz, rows, nz), f32),
            dma((rounds, 6)),
            dma((rounds, 6)),
            dma((4, peers)),
            dma((4, peers)),
            dma((4, peers)),
            dma((4, peers)),
            dma((2,)),
        ],
        compiler_params=pltpu.CompilerParams(
            collective_id=0, has_side_effects=True, vmem_limit_bytes=60 * 1024 * 1024
        ),
    )(couplings, diagonal, right_side, guess)


def solution(mesh):
    dims = (mesh.shape["gx"], mesh.shape["gy"], mesh.shape["gz"])
    cores = 2 if dims[2] % 2 == 0 else 1
    spec = P(None, "gx", "gy", "gz")
    return jax.shard_map(
        functools.partial(per_device, dims, cores),
        mesh=mesh,
        in_specs=(spec,) * 4,
        out_specs=spec,
        check_vma=False,
    )
```

time: 475 us -> 49 us (0.10)
  the two profiles are of different devices: /device:TPU:30 before, /device:TPU:0 now
where the time goes in v1:
time: 49 us; the launch traced here: 48.8 us
  Pallas kernels  47.2 us (96%)
  local copies, waits for them, and re-layouts  1.54 us (3%)
    pallas_call x1, Pallas kernels, per_device(): pl.pallas_call(functools.partial(kernel, dims, cores), out_shape=jax.Shap...  47.2 us
    unnamed x1, local copies, waits for them, and re-layouts  1.54 us

profile of v1, /device:TPU:0, one launch (start us, length us, event | category | flops | bytes accessed | tf_op | source)
XLA Modules:
  0.0 48.8 jit_solution(16918049443415726527)
XLA Ops:
  0.0 47.2 %shard_map.46 = f32[3,8,8,128]{3,2,1,0:T(8,128)} custom-call(f32[18,8,8,128]{3,2,1,0:T(8,128)} %w_ref.1, f32[3,8,8,128]{3,2,1,0:T(8,128)} %d_ref.1, f32[3,8,8,128]{3,2,1,0:T(8,128)} %b_ref.1, f32[3,8,8,128]{3,2,1,0:T(8,128)} %g_ref.1), custom_call_target="tpu_custom_call" | custom-call | tf_op jit(solution)/shard_map/pallas_call | solution.py:470
  47.3 1.5 %copy.6 = f32[3,8,8,128]{3,2,1,0:T(8,128)} copy(f32[3,8,8,128]{3,2,1,0:T(8,128)} %shard_map.46) | data formatting | bytes 196608

commit v2 on v1

--- a/solution.py
+++ b/solution.py
@@ -28,7 +28,7 @@
 def kernel(
     dims, cores, w_ref, d_ref, b_ref, g_ref, out_ref,
     field, halo_x, halo_y, pack_s, pack_r, tot0, c0, w1, tot1, c1, b1,
-    wsend, wall, bsend, ball, e2,
+    wsend, wall, bsend, ball, e2, lines,
     s_sem, r_sem, ws_sem, wr_sem, bs_sem, br_sem, l_sem,
 ):
     ngx, ngy, ngz = dims
@@ -38,7 +38,7 @@
     nX = ngz // cores
     gx, gy, gz = lax.axis_index("gx"), lax.axis_index("gy"), lax.axis_index("gz")
     X, core = gz // cores, gz % cores
-    row = gx * ngy + gy
+    row = gy * ngx + gx
     axes = (("gx", gx, ngx), ("gy", gy, ngy), ("gz", gz, ngz))
 
     def device(name, index):
@@ -47,11 +47,24 @@
         return (here["gx"], here["gy"], here["gz"])
 
     barrier = pltpu.get_barrier_semaphore()
+    close = ngy <= 4 and ngz <= 4
+    awaited = 0
     for name, index, count in axes:
-        for step in range(1, count):
-            pl.semaphore_signal(
-                barrier, inc=1, device_id=device(name, (index + step) % count), device_id_type=MESH
-            )
+        if close and name != "gx":
+            for step in (-1, 1):
+                @pl.when((index + step >= 0) & (index + step < count))
+                def _():
+                    pl.semaphore_signal(
+                        barrier, inc=1, device_id=device(name, jnp.clip(index + step, 0, count - 1)),
+                        device_id_type=MESH,
+                    )
+            awaited = awaited + (index > 0).astype(jnp.int32) + (index < count - 1).astype(jnp.int32)
+        else:
+            for step in range(1, count):
+                pl.semaphore_signal(
+                    barrier, inc=1, device_id=device(name, (index + step) % count), device_id_type=MESH
+                )
+            awaited = awaited + (count - 1)
 
     rounds = field.shape[0]
     for name, index, count in axes:
@@ -69,7 +82,7 @@
                     else:
                         pack_r[r, side] = jnp.zeros(pack_r.shape[2:], jnp.float32)
 
-    pl.semaphore_wait(barrier, ngx + ngy + ngz - 3)
+    pl.semaphore_wait(barrier, awaited)
 
     lane2 = iota((ny, nz), 1)
 
@@ -190,13 +203,13 @@
     def stage(number, small, whole, ss, rs):
         made = []
         if number == 0:
+            for step in range(1, ngx):
+                made.append((small.at[:, pl.ds(0, 1)], whole.at[X, core, :, pl.ds(row, 1)],
+                             step, device("gx", (gx + step) % ngx)))
+        elif number == 1:
+            block = whole.at[X, core, :, pl.ds(gy * ngx, ngx)]
             for step in range(1, ngy):
-                made.append((small.at[:, pl.ds(0, 1)], whole.at[X, core, :, pl.ds(row, 1)],
-                             step, device("gy", (gy + step) % ngy)))
-        elif number == 1:
-            block = whole.at[X, core, :, pl.ds(gx * ngy, ngy)]
-            for step in range(1, ngx):
-                made.append((block, block, step, device("gx", (gx + step) % ngx)))
+                made.append((block, block, step, device("gy", (gy + step) % ngy)))
         elif number == 2:
             block = whole.at[X, core]
             for step in range(1, nX):
@@ -214,7 +227,22 @@
         ]
 
     wargs = (wsend, wall, ws_sem, wr_sem)
-    bargs = (bsend, ball, bs_sem, br_sem)
+
+    def everyone():
+        made = []
+        for az in range(ngz):
+            for ay in range(ngy):
+                for ax in range(ngx):
+                    if ax + ay + az == 0:
+                        continue
+                    made.append(pltpu.make_async_remote_copy(
+                        src_ref=bsend.at[:, pl.ds(0, 1)],
+                        dst_ref=ball.at[X, core, :, pl.ds(row, 1)],
+                        send_sem=bs_sem, recv_sem=br_sem,
+                        device_id=((gx + ax) % ngx, (gy + ay) % ngy, (gz + az) % ngz),
+                        device_id_type=MESH,
+                    ))
+        return made
 
     def start(number, args):
         for copy in stage(number, *args):
@@ -261,11 +289,11 @@
     v = smooth0(0, v)
     send(1, v, nx, 1)
     receive(1, nx, 1)
-    v = smooth0(1, v)
-    send(2, v, nx, 1)
     own(wsend, wall, l_sem.at[0]).wait()
     finish(0, wargs)
     start(1, wargs)
+    v = smooth0(1, v)
+    send(2, v, nx, 1)
     receive(2, nx, 1)
     u = []
     for e in range(EQ):
@@ -275,26 +303,27 @@
         u.append(c1[e] * b)
     half = nx // 2
     send(3, u, half, 2)
-    finish(1, wargs)
-    start(2, wargs)
     receive(3, half, 2)
     u = smooth1(3, u)
+    finish(1, wargs)
     send(4, u, half, 2)
+    start(2, wargs)
+    receive(4, half, 2)
+    for e in range(EQ):
+        rest = b1[e] - tot1[e] * u[e] + near_sum(4, u, e, half, 2, weight1)
+        bsend[e] = to_rows(coarsen(rest, 2)[None])[0]
+    for copy in everyone():
+        copy.start()
+    own(bsend, ball, br_sem).start()
     finish(2, wargs)
     start(3, wargs)
-    receive(4, half, 2)
-    for e in range(EQ):
-        rest = b1[e] - tot1[e] * u[e] + near_sum(4, u, e, half, 2, weight1)
-        bsend[e] = to_rows(coarsen(rest, 2)[None])[0]
-    own(bsend, ball, l_sem.at[1]).start()
-    start(0, bargs)
     finish(3, wargs)
 
     shape = (ngz, rows, nz)
     r_i, l_i = iota(shape, 1), iota(shape, 2)
     g_i = iota(shape, 0)
     zi, yi, xi = l_i % qz, (l_i // qz) % qy, l_i // (qz * qy)
-    gyi, gxi = r_i % ngy, r_i // ngy
+    gyi, gxi = r_i // ngx, r_i % ngx
     inside = [
         ~((xi == qx - 1) & (gxi == ngx - 1)), ~((xi == 0) & (gxi == 0)),
         ~((yi == qy - 1) & (gyi == ngy - 1)), ~((yi == 0) & (gyi == 0)),
@@ -313,10 +342,10 @@
     def near2(v):
         sy, sx = qz, qz * qy
         return [
-            jnp.where(xi == qx - 1, roll(roll(v, (qx - 1) * sx, 2), -ngy, 1), roll(v, -sx, 2)),
-            jnp.where(xi == 0, roll(roll(v, -(qx - 1) * sx, 2), ngy, 1), roll(v, sx, 2)),
-            jnp.where(yi == qy - 1, roll(roll(v, (qy - 1) * sy, 2), -1, 1), roll(v, -sy, 2)),
-            jnp.where(yi == 0, roll(roll(v, -(qy - 1) * sy, 2), 1, 1), roll(v, sy, 2)),
+            jnp.where(xi == qx - 1, roll(roll(v, (qx - 1) * sx, 2), -1, 1), roll(v, -sx, 2)),
+            jnp.where(xi == 0, roll(roll(v, -(qx - 1) * sx, 2), 1, 1), roll(v, sx, 2)),
+            jnp.where(yi == qy - 1, roll(roll(v, (qy - 1) * sy, 2), -ngx, 1), roll(v, -sy, 2)),
+            jnp.where(yi == 0, roll(roll(v, -(qy - 1) * sy, 2), ngx, 1), roll(v, sy, 2)),
             jnp.where(zi == qz - 1, roll(next_of(v), qz - 1, 2), roll(v, -1, 2)),
             jnp.where(zi == 0, roll(prev_of(v), -(qz - 1), 2), roll(v, 1, 2)),
         ]
@@ -339,7 +368,7 @@
     shape3 = (tiles, rows, nz)
     r3, l3, t3 = iota(shape3, 1), iota(shape3, 2), iota(shape3, 0)
     inside3 = [
-        r3 // ngy < ngx - 1, r3 // ngy > 0, r3 % ngy < ngy - 1, r3 % ngy > 0,
+        r3 % ngx < ngx - 1, r3 % ngx > 0, r3 // ngx < ngy - 1, r3 // ngx > 0,
         ~((l3 >= nz - 2) & (t3 == tiles - 1)), ~((l3 < 2) & (t3 == 0)),
     ]
 
@@ -367,7 +396,7 @@
         else:
             up = jnp.where(l3 >= nz - 2, roll(next_of(v), -2, 2), roll(v, -2, 2))
             down = jnp.where(l3 < 2, roll(prev_of(v), 2, 2), roll(v, 2, 2))
-        return [roll(v, -ngy, 1), roll(v, ngy, 1), roll(v, -1, 1), roll(v, 1, 1), up, down]
+        return [roll(v, -1, 1), roll(v, 1, 1), roll(v, -ngx, 1), roll(v, ngx, 1), up, down]
 
     w2, t2, w3, t3s = [], [], [], []
     for e in range(EQ):
@@ -387,11 +416,7 @@
     c2 = [DAMP / t for t in t2]
     c3 = [DAMP / t for t in t3s]
 
-    own(bsend, ball, l_sem.at[1]).wait()
-    finish(0, bargs)
-    for number in range(1, 4):
-        start(number, bargs)
-        finish(number, bargs)
+    pltpu.make_async_copy(ball, ball, br_sem).wait()
 
     keep = 1.0 - DAMP
     for e in range(EQ):
@@ -413,22 +438,49 @@
     source = iota((nz, wide), 0)
     target = iota((nz, wide), 1)
     widen = jnp.where(source == (target // nz) * qz + (target % nz) // 4, 1.0, 0.0).astype(jnp.float32)
-    back = jnp.concatenate(
-        [jnp.broadcast_to(e2[e, gz, pl.ds(row, 1), :], (ny, nz)) for e in range(EQ)], axis=0
-    )
-    back = jnp.dot(back, widen, precision=HIGH, preferred_element_type=jnp.float32)
+    around = [(gx, gy, gz, None)]
+    for axis, index, count in ((0, gx, ngx), (1, gy, ngy), (2, gz, ngz)):
+        for step in (-1, 1):
+            at = [gx, gy, gz]
+            at[axis] = jnp.clip(index + step, 0, count - 1)
+            has = index > 0 if step < 0 else index < count - 1
+            around.append((at[0], at[1], at[2], has))
+    for e in range(EQ):
+        for j, (ax, ay, az, has) in enumerate(around):
+            line = e2[e, az, pl.ds(ay * ngx + ax, 1), :]
+            if has is not None:
+                line = jnp.where(has, line, 0.0)
+            lines[e * 7 + j : e * 7 + j + 1, :] = line
+    for j in range(EQ * 7, lines.shape[0]):
+        lines[j : j + 1, :] = jnp.zeros((1, nz), jnp.float32)
+    back = jnp.dot(lines[...], widen, precision=HIGH, preferred_element_type=jnp.float32)
     ysel = iota((ny, nz), 0) // 4
-    for e in range(EQ):
-        planes = []
+
+    def strip(e, j, x, y):
+        col = (x * qy + y) * nz
+        return jnp.broadcast_to(back[e * 7 + j : e * 7 + j + 1, col : col + nz], (ny, nz))
+
+    def plane(e, j, x):
+        got = strip(e, j, x, 0)
+        for y in range(1, qy):
+            got = jnp.where(ysel == y, strip(e, j, x, y), got)
+        return got
+
+    low, high = pack_r[4, 0], pack_r[4, 1]
+    for e in range(EQ):
+        halo_x[5, 0, e] = halo_x[4, 0, e] + plane(e, 1, qx - 1)
+        halo_x[5, 1, e] = halo_x[4, 1, e] + plane(e, 2, 0)
         for x in range(qx):
-            got = back[e * ny : (e + 1) * ny, (x * qy) * nz : (x * qy + 1) * nz]
-            for y in range(1, qy):
-                col = (x * qy + y) * nz
-                got = jnp.where(ysel == y, back[e * ny : (e + 1) * ny, col : col + nz], got)
-            planes.append(got)
-        u[e] = u[e] + spread(jnp.stack(planes))
-    send(5, u, half, 2)
-    receive(5, half, 2)
+            edge = jnp.where(ysel < qy // 2, strip(e, 3, x, qy - 1), strip(e, 4, x, 0))
+            below, above = plane(e, 5, x), plane(e, 6, x)
+            for i in (2 * x, 2 * x + 1):
+                halo_y[5, e, i] = halo_y[4, e, i] + edge
+                here = lane2 == e * half + i
+                low = jnp.where(here, low + jnp.broadcast_to(below[:, nz - 1 : nz], (ny, nz)), low)
+                high = jnp.where(here, high + jnp.broadcast_to(above[:, 0:1], (ny, nz)), high)
+        u[e] = u[e] + spread(jnp.stack([plane(e, 0, x) for x in range(qx)]))
+    pack_r[5, 0] = low
+    pack_r[5, 1] = high
     u = smooth1(5, u)
     send(6, u, half, 2)
     receive(6, half, 2)
@@ -444,15 +496,18 @@
         out_ref[e] = v[e]
 
     for r in range(rounds):
+        if r == 5:
+            continue
         n, s = (half, 2) if 3 <= r <= 6 else (nx, 1)
         for copy, has_target, _ in copies(r, n, s):
             @pl.when(has_target)
             def _():
                 copy.wait_send()
-    for args in (wargs, bargs):
-        for number in range(4):
-            for copy in stage(number, *args):
-                copy.wait_send()
+    for number in range(4):
+        for copy in stage(number, *wargs):
+            copy.wait_send()
+    for copy in everyone():
+        copy.wait_send()
 
 
 def per_device(dims, cores, couplings, diagonal, right_side, guess):
@@ -489,13 +544,14 @@
             vmem((EQ, ny, nz), f32),
             vmem((nX, cores, EQ, rows, nz), f32),
             vmem((EQ, ngz, rows, nz), f32),
+            vmem((-(-EQ * 7 // 8) * 8, nz), f32),
             dma((rounds, 6)),
             dma((rounds, 6)),
             dma((4, peers)),
             dma((4, peers)),
-            dma((4, peers)),
-            dma((4, peers)),
-            dma((2,)),
+            dma,
+            dma,
+            dma((1,)),
         ],
         compiler_params=pltpu.CompilerParams(
             collective_id=0, has_side_effects=True, vmem_limit_bytes=60 * 1024 * 1024

time: 49 us -> 41 us (0.84)
  Pallas kernels: 47.2 us -> 39.3 us
    pallas_call x1, Pallas kernels: 47.2 us -> 39.3 us  [per_device(): pl.pallas_call(functools.partial(kernel, dims, cores), out_shape=jax.Shap...]
where the time goes in v2:
time: 41 us; the launch traced here: 40.9 us
  Pallas kernels  39.3 us (96%)
  local copies, waits for them, and re-layouts  1.54 us (4%)
    pallas_call x1, Pallas kernels, per_device(): pl.pallas_call(functools.partial(kernel, dims, cores), out_shape=jax.Shap...  39.3 us
    unnamed x1, local copies, waits for them, and re-layouts  1.54 us

profile of v2, /device:TPU:0, one launch (start us, length us, event | category | flops | bytes accessed | tf_op | source)
XLA Modules:
  0.0 40.9 jit_solution(4841158393620067675)
XLA Ops:
  0.0 39.3 %shard_map.46 = f32[3,8,8,128]{3,2,1,0:T(8,128)} custom-call(f32[18,8,8,128]{3,2,1,0:T(8,128)} %w_ref.1, f32[3,8,8,128]{3,2,1,0:T(8,128)} %d_ref.1, f32[3,8,8,128]{3,2,1,0:T(8,128)} %b_ref.1, f32[3,8,8,128]{3,2,1,0:T(8,128)} %g_ref.1), custom_call_target="tpu_custom_call" | custom-call | tf_op jit(solution)/shard_map/pallas_call | solution.py:525
  39.3 1.5 %copy.6 = f32[3,8,8,128]{3,2,1,0:T(8,128)} copy(f32[3,8,8,128]{3,2,1,0:T(8,128)} %shard_map.46) | data formatting | bytes 196608

commit v3 on v2

--- a/solution.py
+++ b/solution.py
@@ -112,54 +112,78 @@
                         device_id=device(name, jnp.clip(target, 0, count - 1)),
                         device_id_type=MESH,
                     ),
-                    has_target, has_source,
+                    has_target, has_source, name,
                 ))
         return made
 
     def send(r, value, n, s):
+        made = copies(r, n, s)
+        if r > 0:
+            for e in range(EQ):
+                field[r, e, 0:n] = value[e]
+        for copy, has_target, _, name in made:
+            if name != "gz":
+                @pl.when(has_target)
+                def _():
+                    copy.start()
         low = jnp.zeros((ny, nz), jnp.float32)
         high = jnp.zeros((ny, nz), jnp.float32)
         for e in range(EQ):
-            if r > 0:
-                field[r, e, 0:n] = value[e]
             for i in range(n):
                 here = lane2 == e * n + i
                 low = jnp.where(here, jnp.broadcast_to(value[e][i, :, 0:1], (ny, nz)), low)
                 high = jnp.where(here, jnp.broadcast_to(value[e][i, :, nz - 1 : nz], (ny, nz)), high)
         pack_s[r, 0] = low
         pack_s[r, 1] = high
-        for copy, has_target, _ in copies(r, n, s):
-            @pl.when(has_target)
-            def _():
-                copy.start()
+        for copy, has_target, _, name in made:
+            if name == "gz":
+                @pl.when(has_target)
+                def _():
+                    copy.start()
 
     def receive(r, n, s):
-        for copy, _, has_source in copies(r, n, s):
+        for copy, _, has_source, _ in copies(r, n, s):
             @pl.when(has_source)
             def _():
                 copy.wait_recv()
 
-    def near_sum(r, value, e, n, s, weight):
-        v = value[e]
+    def before(v, e, n, s, weight, base, scale):
         shape = (n, ny, nz)
         y, z = iota(shape, 1), iota(shape, 2)
-        hy = halo_y[r, e, 0:n]
+        edge = jnp.zeros((1, ny, nz), jnp.float32)
+        near = [
+            jnp.concatenate([v[1:], edge], axis=0),
+            jnp.concatenate([edge, v[:-1]], axis=0),
+            jnp.where(y >= ny - s, 0.0, roll(v, -s, 1)),
+            jnp.where(y < s, 0.0, roll(v, s, 1)),
+            jnp.where(z >= nz - s, 0.0, roll(v, -s, 2)),
+            jnp.where(z < s, 0.0, roll(v, s, 2)),
+        ]
+        w = [weight(e, k) for k in range(6)]
+        total = w[0] * near[0]
+        for k in range(1, 6):
+            total = total + w[k] * near[k]
+        wy = jnp.where(y >= ny - s, w[2], jnp.where(y < s, w[3], 0.0))
+        wz = jnp.where(z >= nz - s, w[4], jnp.where(z < s, w[5], 0.0))
+        up, down = w[0][n - 1], w[1][0]
+        if scale is not None:
+            total, wy, wz = scale * total, scale * wy, scale * wz
+            up, down = scale[n - 1] * up, scale[0] * down
+        return base + total, up, down, wy, wz
+
+    def after(r, e, n, s, ready):
+        total, up, down, wy, wz = ready
+        shape = (n, ny, nz)
+        y, z = iota(shape, 1), iota(shape, 2)
         low = pack_r[r, 0]
         high = pack_r[r, 1]
         zl = jnp.stack([jnp.broadcast_to(low[:, e * n + i : e * n + i + 1], (ny, nz)) for i in range(n)])
         zh = jnp.stack([jnp.broadcast_to(high[:, e * n + i : e * n + i + 1], (ny, nz)) for i in range(n)])
-        near = [
-            jnp.concatenate([v[1:], halo_x[r, 1, e][None]], axis=0),
-            jnp.concatenate([halo_x[r, 0, e][None], v[:-1]], axis=0),
-            jnp.where(y >= ny - s, hy, roll(v, -s, 1)),
-            jnp.where(y < s, hy, roll(v, s, 1)),
-            jnp.where(z >= nz - s, zh, roll(v, -s, 2)),
-            jnp.where(z < s, zl, roll(v, s, 2)),
-        ]
-        total = weight(e, 0) * near[0]
-        for k in range(1, 6):
-            total = total + weight(e, k) * near[k]
-        return total
+        hy = jnp.where((y < s) | (y >= ny - s), halo_y[r, e, 0:n], 0.0)
+        total = total + wy * hy + wz * jnp.where(z < s, zl, zh)
+        first = total[0] + down * halo_x[r, 0, e]
+        last = total[n - 1] + up * halo_x[r, 1, e]
+        return jnp.concatenate([first[None], total[1 : n - 1], last[None]], axis=0)
 
     def coarsen(a, s):
         n = a.shape[0]
@@ -273,45 +297,45 @@
     own(wsend, wall, l_sem.at[0]).start()
     start(0, wargs)
 
-    def smooth0(r, v):
-        return [
-            (1.0 - DAMP) * v[e] + c0[e] * (b_ref[e] + near_sum(r, v, e, nx, 1, weight0))
+    keep = 1.0 - DAMP
+
+    def apply(r, v, n, s, weight, base, scale):
+        ready = [
+            before(v[e], e, n, s, weight, base(e), None if scale is None else scale[e])
             for e in range(EQ)
         ]
+        if r != 5:
+            receive(r, n, s)
+        return [after(r, e, n, s, ready[e]) for e in range(EQ)]
+
+    def smooth0(r, v):
+        return apply(r, v, nx, 1, weight0, lambda e: keep * v[e] + c0[e] * b_ref[e], c0)
 
     def smooth1(r, v):
-        return [
-            (1.0 - DAMP) * v[e] + c1[e] * (b1[e] + near_sum(r, v, e, nx // 2, 2, weight1))
-            for e in range(EQ)
-        ]
-
-    receive(0, nx, 1)
+        return apply(r, v, nx // 2, 2, weight1, lambda e: keep * v[e] + c1[e] * b1[e], c1)
+
     v = smooth0(0, v)
     send(1, v, nx, 1)
-    receive(1, nx, 1)
+    v = smooth0(1, v)
     own(wsend, wall, l_sem.at[0]).wait()
     finish(0, wargs)
+    send(2, v, nx, 1)
     start(1, wargs)
-    v = smooth0(1, v)
-    send(2, v, nx, 1)
-    receive(2, nx, 1)
     u = []
-    for e in range(EQ):
-        rest = b_ref[e] - tot0[e] * v[e] + near_sum(2, v, e, nx, 1, weight0)
-        b = coarsen(rest, 1)
+    rest = apply(2, v, nx, 1, weight0, lambda e: b_ref[e] - tot0[e] * v[e], None)
+    for e in range(EQ):
+        b = coarsen(rest[e], 1)
         b1[e] = b
         u.append(c1[e] * b)
     half = nx // 2
     send(3, u, half, 2)
-    receive(3, half, 2)
     u = smooth1(3, u)
     finish(1, wargs)
     send(4, u, half, 2)
     start(2, wargs)
-    receive(4, half, 2)
-    for e in range(EQ):
-        rest = b1[e] - tot1[e] * u[e] + near_sum(4, u, e, half, 2, weight1)
-        bsend[e] = to_rows(coarsen(rest, 2)[None])[0]
+    rest = apply(4, u, half, 2, weight1, lambda e: b1[e] - tot1[e] * u[e], None)
+    for e in range(EQ):
+        bsend[e] = to_rows(coarsen(rest[e], 2)[None])[0]
     for copy in everyone():
         copy.start()
     own(bsend, ball, br_sem).start()
@@ -418,7 +442,6 @@
 
     pltpu.make_async_copy(ball, ball, br_sem).wait()
 
-    keep = 1.0 - DAMP
     for e in range(EQ):
         rhs = whole(ball, e)
         v2 = c2[e] * rhs
@@ -483,14 +506,11 @@
     pack_r[5, 1] = high
     u = smooth1(5, u)
     send(6, u, half, 2)
-    receive(6, half, 2)
     u = smooth1(6, u)
     v = [field[2, e] + spread(u[e]) for e in range(EQ)]
     send(7, v, nx, 1)
-    receive(7, nx, 1)
     v = smooth0(7, v)
     send(8, v, nx, 1)
-    receive(8, nx, 1)
     v = smooth0(8, v)
     for e in range(EQ):
         out_ref[e] = v[e]
@@ -499,7 +519,7 @@
         if r == 5:
             continue
         n, s = (half, 2) if 3 <= r <= 6 else (nx, 1)
-        for copy, has_target, _ in copies(r, n, s):
+        for copy, has_target, _, _ in copies(r, n, s):
             @pl.when(has_target)
             def _():
                 copy.wait_send()

time: 41 us -> 39.4 us (0.961)
  Pallas kernels: 39.3 us -> 37.7 us
    pallas_call x1, Pallas kernels: 39.3 us -> 37.7 us  [per_device(): pl.pallas_call(functools.partial(kernel, dims, cores), out_shape=jax.Shap...]
where the time goes in v3:
time: 39.4 us; the launch traced here: 39.2 us
  Pallas kernels  37.7 us (96%)
  local copies, waits for them, and re-layouts  1.54 us (4%)
    pallas_call x1, Pallas kernels, per_device(): pl.pallas_call(functools.partial(kernel, dims, cores), out_shape=jax.Shap...  37.7 us
    unnamed x1, local copies, waits for them, and re-layouts  1.54 us

profile of v3, /device:TPU:0, one launch (start us, length us, event | category | flops | bytes accessed | tf_op | source)
XLA Modules:
  0.0 39.2 jit_solution(10666556350973031534)
XLA Ops:
  0.0 37.7 %shard_map.46 = f32[3,8,8,128]{3,2,1,0:T(8,128)} custom-call(f32[18,8,8,128]{3,2,1,0:T(8,128)} %w_ref.1, f32[3,8,8,128]{3,2,1,0:T(8,128)} %d_ref.1, f32[3,8,8,128]{3,2,1,0:T(8,128)} %b_ref.1, f32[3,8,8,128]{3,2,1,0:T(8,128)} %g_ref.1), custom_call_target="tpu_custom_call" | custom-call | tf_op jit(solution)/shard_map/pallas_call | solution.py:545
  37.7 1.5 %copy.6 = f32[3,8,8,128]{3,2,1,0:T(8,128)} copy(f32[3,8,8,128]{3,2,1,0:T(8,128)} %shard_map.46) | data formatting | bytes 196608

commit v4 on v3

--- a/solution.py
+++ b/solution.py
@@ -334,9 +334,8 @@
     send(4, u, half, 2)
     start(2, wargs)
     rest = apply(4, u, half, 2, weight1, lambda e: b1[e] - tot1[e] * u[e], None)
-    for e in range(EQ):
-        bsend[e] = to_rows(coarsen(rest[e], 2)[None])[0]
-    for copy in everyone():
+    bsend[...] = to_rows(jnp.stack([coarsen(rest[e], 2) for e in range(EQ)]))
+    for copy in reversed(everyone()):
         copy.start()
     own(bsend, ball, br_sem).start()
     finish(2, wargs)
@@ -442,20 +441,25 @@
 
     pltpu.make_async_copy(ball, ball, br_sem).wait()
 
-    for e in range(EQ):
-        rhs = whole(ball, e)
-        v2 = c2[e] * rhs
-        for step in range(SWEEPS - 1):
-            v2 = keep * v2 + c2[e] * (rhs + dot_near(w2[e], near2(v2)))
-        rest = rhs - t2[e] * v2 + dot_near(w2[e], near2(v2))
-        rhs3 = join(pair(rest))
-        v3 = c3[e] * rhs3
-        for step in range(COARSE_SWEEPS - 1):
-            v3 = keep * v3 + c3[e] * (rhs3 + dot_near(w3[e], near3(v3)))
-        v2 = v2 + part(v3)
-        for step in range(SWEEPS):
-            v2 = keep * v2 + c2[e] * (rhs + dot_near(w2[e], near2(v2)))
-        e2[e] = v2
+    every = range(EQ)
+    rhs = [whole(ball, e) for e in every]
+
+    def smooth2(v):
+        return [keep * v[e] + c2[e] * (rhs[e] + dot_near(w2[e], near2(v[e]))) for e in every]
+
+    v2 = [c2[e] * rhs[e] for e in every]
+    for step in range(SWEEPS - 1):
+        v2 = smooth2(v2)
+    rest = [rhs[e] - t2[e] * v2[e] + dot_near(w2[e], near2(v2[e])) for e in every]
+    rhs3 = [join(pair(rest[e])) for e in every]
+    v3 = [c3[e] * rhs3[e] for e in every]
+    for step in range(COARSE_SWEEPS - 1):
+        v3 = [keep * v3[e] + c3[e] * (rhs3[e] + dot_near(w3[e], near3(v3[e]))) for e in every]
+    v2 = [v2[e] + part(v3[e]) for e in every]
+    for step in range(SWEEPS):
+        v2 = smooth2(v2)
+    for e in every:
+        e2[e] = v2[e]
 
     wide = groups * nz
     source = iota((nz, wide), 0)

time: 39.4 us -> 39.2 us (level)
  no operation moved by 1% of the time
where the time goes in v4:
time: 39.2 us; the launch traced here: 39.1 us
  Pallas kernels  37.5 us (96%)
  local copies, waits for them, and re-layouts  1.54 us (4%)
    pallas_call x1, Pallas kernels, per_device(): pl.pallas_call(functools.partial(kernel, dims, cores), out_shape=jax.Shap...  37.5 us
    unnamed x1, local copies, waits for them, and re-layouts  1.54 us

profile of v4, /device:TPU:0, one launch (start us, length us, event | category | flops | bytes accessed | tf_op | source)
XLA Modules:
  0.0 39.1 jit_solution(10674775428747800221)
XLA Ops:
  0.0 37.5 %shard_map.46 = f32[3,8,8,128]{3,2,1,0:T(8,128)} custom-call(f32[18,8,8,128]{3,2,1,0:T(8,128)} %w_ref.1, f32[3,8,8,128]{3,2,1,0:T(8,128)} %d_ref.1, f32[3,8,8,128]{3,2,1,0:T(8,128)} %b_ref.1, f32[3,8,8,128]{3,2,1,0:T(8,128)} %g_ref.1), custom_call_target="tpu_custom_call" | custom-call | tf_op jit(solution)/shard_map/pallas_call | solution.py:549
  37.5 1.5 %copy.6 = f32[3,8,8,128]{3,2,1,0:T(8,128)} copy(f32[3,8,8,128]{3,2,1,0:T(8,128)} %shard_map.46) | data formatting | bytes 196608
